TPU v7x, 32 devices: a whole 2x2x4 slice. The times are simulated.
32 devices in a mesh: group: 16 (over z, y, core), mp: 2 (over x).
Axes of the slice: x: 2, y: 2, z: 4, core: 2. Of those that a mesh axis runs over, the one named last changes fastest.
Arguments:
- hidden: bfloat16 [8192, 2048], P('group'), may hold values from -12 to 12
- ln_gain: float32 [2048], replicated, may hold values from 0.5 to 1.5
- ln_shift: float32 [2048], replicated, may hold values from -2 to 2
- qkv_weight: bfloat16 [3, 2048, 1024], P(None, None, 'mp'), may hold values from -0.25 to 0.25
- qkv_bias: float32 [3, 1024], P(None, 'mp'), may hold values from -2 to 2
- out_weight: bfloat16 [1024, 2048], P('mp'), may hold values from -0.1875 to 0.1875
- up_weight: bfloat16 [2048, 4096], P(None, 'mp'), may hold values from -0.125 to 0.125
- up_bias: float32 [4096], P('mp'), may hold values from -3 to 3
- down_weight: bfloat16 [4096, 2048], P('mp'), may hold values from -0.09375 to 0.09375
- branch_bias: float32 [2048], replicated, may hold values from -2 to 2
- next_gain: float32 [2048], replicated, may hold values from 0.5 to 1.5
- next_shift: float32 [2048], replicated, may hold values from -2 to 2
- next_weight: bfloat16 [3, 2048, 1024], P(None, None, 'mp'), may hold values from -0.125 to 0.125
- next_bias: float32 [3, 1024], P(None, 'mp'), may hold values from -2 to 2
- key_cache: bfloat16 [128, 384, 1024], P('group', None, 'mp'), may hold values from -70 to 70
- value_cache: bfloat16 [128, 384, 1024], P('group', None, 'mp'), may hold values from -6 to 6
- tail_keys: bfloat16 [32, 2048, 1024], P('group', None, 'mp'), may hold values from -70 to 70
- tail_values: bfloat16 [32, 2048, 1024], P('group', None, 'mp'), may hold values from -6 to 6
- lengths: int32 [128], P('group'), may hold values from 1 to 384, as said below
- split_slot: int32 [32], P('group'), may hold values from 0 to 7, as said below
- tail_len: int32 [32], replicated, may hold values from 1 to 2048, as said below
- parents: int32 [8192], P('group'), may hold values from 0 to 63, as said below
- accepted: int32 [128, 8], P('group'), may hold values from 0 to 63, as said below
Outputs:
- new_hidden: bfloat16 [8192, 2048], P(('group', 'mp'))
- next_qkv: bfloat16 [3, 8192, 1024], P(None, 'group', 'mp')
- accepted_rows: bfloat16 [2, 1024, 1024], P(None, 'group', 'mp')
Inputs may be any that keep to these rules, and one draw needn't show every extreme that they name: `lengths`: positions of each request in its own group; a request named in split_slot holds exactly 384. `split_slot`: distinct requests of the group, by index within the group; rank t continues at rank t of the group whose index differs in the lowest bit. `tail_len`: rank t of group g holds the continuation of the request named at rank t by split_slot of group g xor 1; some continuation holds exactly 2048. `parents`: each token's parent is an earlier token of its request; token 0 of each request names itself. `accepted`: distinct tokens of the request.
All inputs are finite; a program needn't handle non-finite values.
Results may differ from a plain program's by a relative error of at most 0.01.
Values may be sent and summed in bfloat16 or wider, within the bound.
No kernel may reach another device: no remote copies, remote signals or barrier semaphores. Data moves between devices by JAX's collectives and lax.ppermute only.
A program may use at most 192 MiB of HBM per device.

v0:
```python
import functools
from types import SimpleNamespace

import jax
import jax.numpy as jnp
import numpy as np
from jax import lax
from jax.experimental import pallas as pl
from jax.experimental.pallas import tpu as pltpu
from jax.sharding import PartitionSpec as P

HD = 64
ROT = 32
DRAFT = 64
PAIR = 128
BLOCK = 512
STEP = 16

KEPT = tuple(dict(w_qkv=0, w_up=0, w_down=0, w_out=0))
FREE = tuple(dict(far_keys=0, far_values=0)) + tuple(range(20))

epsilon = 1e-05
very_low = -1e30

HBM = pltpu.HBM
VMEM = pltpu.VMEM
SMEM = pltpu.SMEM
I32 = jnp.int32
F32 = jnp.float32
BF16 = jnp.bfloat16

CHUNKS = (((0, 1),), ((2, 3),), ((4, 5),), ((6,), (7,)))
FINISHES = ((0, 3), (3, 4), (4, 5))


def dot(a, b):
    return jnp.dot(a, b, preferred_element_type=F32)


def dot_nt(a, b):
    return lax.dot_general(a, b, (((1,), (1,)), ((), ())), preferred_element_type=F32)


def request_at(place, slots, requests):
    tails = slots.shape[0]
    whole = requests - tails
    if place >= whole:
        return slots[place - whole]
    ordered = [slots[t] for t in range(tails)]
    for end in range(tails - 1, 0, -1):
        for t in range(end):
            low = jnp.minimum(ordered[t], ordered[t + 1])
            high = jnp.maximum(ordered[t], ordered[t + 1])
            ordered[t], ordered[t + 1] = low, high
    request = jnp.int32(place)
    for slot in ordered:
        request = request + (request >= slot).astype(I32)
    return request


class Copies:
    def __init__(self, sems):
        self.sems = sems
        self.used = 0

    def make(self, source, target):
        copy = pltpu.make_async_copy(source, target, self.sems.at[self.used])
        self.used += 1
        return copy

    def start(self, source, target):
        copy = self.make(source, target)
        copy.start()
        return copy


def wait(*copies):
    for copy in copies:
        copy.wait()


def layer_norm(values, gain, shift):
    centred = values - jnp.mean(values, axis=-1, keepdims=True)
    variance = jnp.mean(centred * centred, axis=-1, keepdims=True)
    return centred * lax.rsqrt(variance + epsilon) * gain + shift


def ancestor_pair(parents, first, second):
    lane = lax.broadcasted_iota(I32, (1, PAIR), 1)

    def row_of(request, half):
        row = parents[pl.ds(request // 2, 1), :]
        return jnp.where(request % 2 == half, row, pltpu.roll(row, DRAFT, 1))

    ids = jnp.where(lane < DRAFT, row_of(first, 0), row_of(second, 1) + DRAFT)
    row_id = lax.broadcasted_iota(I32, (PAIR, PAIR), 0)
    col_id = lax.broadcasted_iota(I32, (PAIR, PAIR), 1)
    below = jnp.where(row_id == ids, 1.0, 0.0).astype(BF16)
    same = jnp.where(row_id == col_id, 1.0, 0.0).astype(BF16)
    reach = jnp.minimum(dot_nt(same, below) + same.astype(F32), 1.0)
    for _ in range((DRAFT - 1).bit_length()):
        half = reach.astype(BF16)
        reach = jnp.minimum(dot(half, half), 1.0)
    return reach


def rotary_tables(positions):
    feature = lax.broadcasted_iota(I32, (1, PAIR), 1) % HD
    inverse = jnp.zeros((1, PAIR), F32)
    for k in range(ROT // 2):
        rate = float(np.float32(10000.0 ** (-k * 2.0 / ROT)))
        inverse = jnp.where(feature % (ROT // 2) == k, rate, inverse)
    angles = positions * inverse
    sine = jnp.sin(angles)
    same = jnp.where(feature < ROT, jnp.cos(angles), 1.0)
    ahead = jnp.where(feature < ROT // 2, -sine, 0.0)
    behind = jnp.where((feature >= ROT // 2) & (feature < ROT), sine, 0.0)
    return same, ahead, behind


def rotate(values, tables):
    same, ahead, behind = tables
    half_rot = ROT // 2
    parts = []
    for start in range(0, values.shape[1], PAIR):
        part = values[:, start : start + PAIR]
        parts.append(
            part * same
            + pltpu.roll(part, PAIR - half_rot, 1) * ahead
            + pltpu.roll(part, half_rot, 1) * behind
        )
    return jnp.concatenate(parts, axis=1) if len(parts) > 1 else parts[0]


def gelu(v):
    inner = np.float32(np.sqrt(2.0 / np.pi)) * (v + 0.044715 * (v * v * v))
    return 0.5 * v * (1.0 + jnp.tanh(inner))


def picks(accepted, request, tokens):
    count = accepted.shape[1]
    row = accepted[pl.ds(request, 1), :]
    row_id = lax.broadcasted_iota(I32, (count, count), 0)
    col_id = lax.broadcasted_iota(I32, (count, count), 1)
    ids = jnp.sum(jnp.where(row_id == col_id, row, 0).astype(F32), axis=1, keepdims=True)
    token_id = lax.broadcasted_iota(I32, (count, tokens), 1).astype(F32)
    return jnp.where(token_id == ids, 1.0, 0.0).astype(BF16)


def branch_kernel(pieces, first, names, *refs):
    r = SimpleNamespace(**dict(zip(names, refs)))
    places = [place for piece in pieces for place in piece]
    count = len(places)
    rows = count * DRAFT
    requests, _, width = r.hidden.shape
    heads_width = r.w_qkv.shape[2]
    units = r.w_up.shape[1]
    cap_len = r.key_cache.shape[1]
    tails = r.split_slot.shape[0]
    whole = requests - tails
    group = min(heads_width, 4 * HD)
    per = group // HD
    copies = Copies(r.sems)

    got_scalars = [
        copies.start(r.split_slot, r.slots),
        copies.start(r.lengths, r.own_len),
        copies.start(r.tail_len, r.all_len),
    ]
    got_small = [
        copies.start(r.parents, r.tree),
        copies.start(r.accepted, r.taken),
        copies.start(r.ln_gain, r.gain),
        copies.start(r.ln_shift, r.shift),
        copies.start(r.qkv_bias, r.b_qkv),
        copies.start(r.up_bias, r.b_up),
    ]
    early = places[-1] < whole
    if early:
        span = pl.ds(places[0], places[-1] - places[0] + 1 + tails)
        got_hidden = [copies.start(r.hidden.at[span], r.h)]
    got_qkv = [copies.start(r.qkv_weight.at[c], r.w_qkv.at[c]) for c in range(3)] if first else []
    wait(*got_scalars)
    order = [request_at(place, r.slots, requests) for place in places]
    far_base = jnp.bitwise_xor(lax.axis_index("group"), 1) * tails
    if not early:
        got_hidden = [copies.start(r.hidden.at[order[i]], r.h.at[i]) for i in range(count)]
        rows_of = range(count)
    else:
        rows_of = [request - places[0] for request in order]
    got_own = [
        (
            copies.start(r.key_cache.at[order[i]], r.k_own.at[i]),
            copies.start(r.value_cache.at[order[i]], r.v_own.at[i]),
        )
        for i in range(count)
    ]
    up_blocks = range(0, units, BLOCK)
    down_blocks = range(0, width, BLOCK)
    if first:
        got_up = [
            copies.start(r.up_weight.at[:, pl.ds(b, BLOCK)], r.w_up.at[:, pl.ds(b, BLOCK)])
            for b in up_blocks
        ]
        got_out = copies.start(r.out_weight, r.w_out)
        got_down = [
            copies.start(r.down_weight.at[:, pl.ds(b, BLOCK)], r.w_down.at[:, pl.ds(b, BLOCK)])
            for b in down_blocks
        ]
    if places[-1] >= whole:
        got_far = [
            (copies.start(r.far_keys.at[t], r.k_far.at[t]), copies.start(r.far_values.at[t], r.v_far.at[t]))
            for t in range(tails)
        ]

    wait(*got_small)
    reach = []
    tables = []
    for i in range(0, count, 2):
        both = ancestor_pair(r.tree, order[i], order[i + 1])
        depth = jnp.sum(both, axis=1, keepdims=True) - 1.0
        for k in (0, 1):
            span = slice(k * DRAFT, (k + 1) * DRAFT)
            reach.append(both[span, span])
            base = r.own_len[order[i + k]].astype(F32)
            if places[i + k] >= whole:
                base = base + r.all_len[far_base + places[i + k] - whole].astype(F32)
            tables.append(rotary_tables(base + depth[span]))

    wait(*got_hidden)
    gain = r.gain[...]
    shift = r.shift[...]

    for i in range(count):
        for k in range(0, DRAFT, STEP):
            values = r.h[rows_of[i], pl.ds(k, STEP), :].astype(F32)
            r.normed[pl.ds(i * DRAFT + k, STEP), :] = layer_norm(values, gain, shift).astype(BF16)

    for c, target in enumerate((r.q, r.k, r.v)):
        wait(*got_qkv[c : c + 1])
        linear = dot(r.normed[...], r.w_qkv[c]) + r.b_qkv[pl.ds(c, 1), :]
        for i in range(count):
            part = linear[i * DRAFT : (i + 1) * DRAFT]
            if c < 2:
                part = rotate(part, tables[i])
            part = part.astype(BF16)
            if c == 0:
                part = part * np.float32(HD**-0.5).astype(BF16)
            target[pl.ds(i * DRAFT, DRAFT), :] = part

    writes = []
    for i in range(count):
        hot = picks(r.taken, order[i], DRAFT)
        for c, source in enumerate((r.k, r.v)):
            r.picked[c, i] = dot(hot, source[pl.ds(i * DRAFT, DRAFT), :]).astype(BF16)
            writes.append(copies.start(r.picked.at[c, i], r.rows_out.at[c, order[i]]))

    lane_head = lax.broadcasted_iota(I32, (DRAFT, group), 1) // HD
    for i in range(count):
        wait(*got_own[i])
        t = places[i] - whole
        if t >= 0:
            wait(*got_far[t])
        span = pl.ds(i * DRAFT, DRAFT)
        key_id = lax.broadcasted_iota(I32, (1, cap_len), 1)
        own_bias = jnp.where(key_id < r.own_len[order[i]], 0.0, very_low)
        tree_bias = jnp.where(reach[i] > 0.5, 0.0, very_low)
        tree_bias = jnp.concatenate([tree_bias] * per, axis=0)
        for low in range(0, heads_width, group):
            cols = slice(low, low + group)
            query = r.q[span, cols]
            query = jnp.concatenate(
                [jnp.where(lane_head == h, query, jnp.zeros_like(query)) for h in range(per)], axis=0
            )
            own = dot_nt(query, r.k_own[i, :, cols]) + own_bias
            tree = dot_nt(query, r.k[span, cols]) + tree_bias
            top = jnp.maximum(
                jnp.max(own, axis=1, keepdims=True), jnp.max(tree, axis=1, keepdims=True)
            )
            own = jnp.exp(own - top)
            tree = jnp.exp(tree - top)
            total = jnp.sum(own, axis=1, keepdims=True) + jnp.sum(tree, axis=1, keepdims=True)
            mixed = dot(own.astype(BF16), r.v_own[i, :, cols])
            mixed = mixed + dot(tree.astype(BF16), r.v[span, cols])
            if t >= 0:
                far_cap = r.k_far.shape[1]
                far_len = r.all_len[far_base + t]
                for start in range(0, far_cap, BLOCK):
                    part = slice(start, start + BLOCK)
                    far_id = lax.broadcasted_iota(I32, (1, BLOCK), 1) + start
                    far_bias = jnp.where(far_id < far_len, 0.0, very_low)
                    far = dot_nt(query, r.k_far[t, part, cols]) + far_bias
                    peak = jnp.maximum(top, jnp.max(far, axis=1, keepdims=True))
                    keep = jnp.exp(top - peak)
                    far = jnp.exp(far - peak)
                    total = total * keep + jnp.sum(far, axis=1, keepdims=True)
                    mixed = mixed * keep + dot(far.astype(BF16), r.v_far[t, part, cols])
                    top = peak
            mixed = mixed * (1.0 / total)
            joined = jnp.zeros((DRAFT, group), F32)
            for h in range(per):
                joined = jnp.where(lane_head == h, mixed[h * DRAFT : (h + 1) * DRAFT], joined)
            r.att[span, cols] = joined.astype(BF16)

    for n, b in enumerate(up_blocks):
        if first:
            wait(got_up[n])
        cols = pl.ds(b, BLOCK)
        r.act[:, cols] = gelu(dot(r.normed[...], r.w_up[:, cols]) + r.b_up[:, cols]).astype(BF16)
    if first:
        wait(got_out)
    for n, b in enumerate(down_blocks):
        cols = pl.ds(b, BLOCK)
        summed = dot(r.att[...], r.w_out[:, cols])
        if first:
            wait(got_down[n])
        r.sums[:, cols] = (summed + dot(r.act[...], r.w_down[:, cols])).astype(BF16)
        start = 0
        for piece, target in zip(pieces, (getattr(r, n) for n in names if n.startswith("piece"))):
            size = len(piece) * DRAFT
            writes.append(copies.start(r.sums.at[pl.ds(start, size), cols], target.at[:, cols]))
            start += size
    wait(*writes)


def call(kernel, ins, outs, scratch, aliases, vmem, name):
    names = (*ins, *outs, *scratch)
    results = pl.pallas_call(
        functools.partial(kernel, names),
        out_shape=[(VMEM if key in KEPT else HBM)(shape, BF16) for key, shape in outs.items()],
        in_specs=[
            pl.BlockSpec(memory_space=VMEM if key in KEPT else pl.ANY if key in FREE else HBM) for key in ins
        ],
        out_specs=[pl.BlockSpec(memory_space=VMEM if key in KEPT else HBM) for key in outs],
        scratch_shapes=list(scratch.values()),
        input_output_aliases={list(ins).index(a): list(outs).index(b) for a, b in aliases.items()},
        compiler_params=pltpu.CompilerParams(vmem_limit_bytes=vmem * 2**20),
        name=name,
    )(*(x if key in FREE else pltpu.with_memory_space_constraint(x, VMEM if key in KEPT else HBM) for key, x in ins.items()))
    return SimpleNamespace(**dict(zip(outs, results)))


def branch(pieces, tail, a, before):
    requests, _, width = a.hidden.shape
    heads_width = a.qkv_weight.shape[2]
    units = a.up_weight.shape[1]
    cap_len = a.key_cache.shape[1]
    acc_count = a.accepted.shape[1]
    tails = a.split_slot.shape[0]
    count = sum(len(piece) for piece in pieces)
    rows = count * DRAFT
    ins = dict(
        lengths=a.lengths,
        split_slot=a.split_slot,
        tail_len=a.tail_len,
        accepted=a.accepted,
        parents=a.parents,
        ln_gain=a.ln_gain,
        ln_shift=a.ln_shift,
        qkv_bias=a.qkv_bias,
        up_bias=a.up_bias,
        hidden=a.hidden,
        key_cache=a.key_cache,
        value_cache=a.value_cache,
    )
    scratch = dict(
        slots=SMEM(a.split_slot.shape, I32),
        own_len=SMEM(a.lengths.shape, I32),
        all_len=SMEM(a.tail_len.shape, I32),
        tree=VMEM(a.parents.shape, I32),
        taken=VMEM(a.accepted.shape, I32),
        gain=VMEM((1, width), F32),
        shift=VMEM((1, width), F32),
        b_qkv=VMEM((3, heads_width), F32),
        b_up=VMEM((1, units), F32),
        h=VMEM((count + (0 if tail else tails), DRAFT, width), BF16),
        normed=VMEM((rows, width), BF16),
        k_own=VMEM((count, cap_len, heads_width), BF16),
        v_own=VMEM((count, cap_len, heads_width), BF16),
        q=VMEM((rows, heads_width), BF16),
        k=VMEM((rows, heads_width), BF16),
        v=VMEM((rows, heads_width), BF16),
        att=VMEM((rows, heads_width), BF16),
        act=VMEM((rows, units), BF16),
        sums=VMEM((rows, width), BF16),
        picked=VMEM((2, count, acc_count, heads_width), BF16),
        sems=pltpu.SemaphoreType.DMA((100,)),
    )
    if tail:
        ins.update(far_keys=a.far_keys, far_values=a.far_values)
        scratch.update(k_far=VMEM(a.far_keys.shape, BF16), v_far=VMEM(a.far_values.shape, BF16))
    outs = dict(rows_out=(2, requests, acc_count, heads_width))
    aliases = {}
    if before is None:
        ins.update(
            qkv_weight=a.qkv_weight, up_weight=a.up_weight, down_weight=a.down_weight, out_weight=a.out_weight
        )
        outs.update(
            w_qkv=a.qkv_weight.shape, w_up=a.up_weight.shape, w_down=a.down_weight.shape, w_out=a.out_weight.shape
        )
    else:
        ins.update(
            rows_in=before.rows_out, w_qkv=a.w_qkv, w_up=a.w_up, w_down=a.w_down, w_out=a.w_out
        )
        aliases = dict(rows_in="rows_out")
    sizes = [len(piece) * DRAFT for piece in pieces]
    if len(sizes) == 1:
        outs.update(piece_a=(sizes[0], width))
    else:
        outs.update(piece_a=(sizes[0], width), piece_b=(sizes[1], width))

    def kernel(names, *refs):
        branch_kernel(pieces, before is None, names, *refs)

    out = call(kernel, ins, outs, scratch, aliases, 36, "branch")
    parts = [out.piece_a] if len(sizes) == 1 else [out.piece_a, out.piece_b]
    if before is None:
        a.w_qkv, a.w_up, a.w_down, a.w_out = out.w_qkv, out.w_up, out.w_down, out.w_out
    return parts, out


def finish_kernel(pieces, terms, names, *refs):
    r = SimpleNamespace(**{str(name): ref for name, ref in zip(names, refs)})
    requests, _, width = r.hidden.shape
    share = r.new_hidden.shape[0]
    places = [place for piece in pieces for place in piece]
    count = len(places)
    copies = Copies(r.sems)
    wait_slots = copies.start(r.split_slot, r.slots)
    got_terms = []
    given = iter(refs)
    for n in range(terms):
        start = 0
        for piece in pieces:
            size = len(piece) * DRAFT
            got_terms.append(copies.start(next(given), r.t.at[n, pl.ds(start, size)]))
            start += size
    got_small = [
        copies.start(r.branch_bias, r.bias),
        copies.start(r.next_gain, r.gain),
        copies.start(r.next_shift, r.shift),
        copies.start(r.next_bias, r.b),
    ]
    wait(wait_slots)
    order = [request_at(place, r.slots, requests) for place in places]
    got_hidden = [
        copies.start(r.hidden.at[order[i]], r.h.at[pl.ds(i * DRAFT, DRAFT)]) for i in range(count)
    ]
    got_w = [copies.start(r.next_weight.at[c], r.w.at[c]) for c in range(3)]
    wait(*got_terms, *got_small, *got_hidden)
    bias = r.bias[...]
    gain = r.gain[...]
    shift = r.shift[...]

    def body(k, carry):
        at = pl.ds(pl.multiple_of(k * STEP, STEP), STEP)
        summed = r.t[0, at, :].astype(F32)
        for n in range(1, terms):
            summed = summed + r.t[n, at, :].astype(F32)
        new = (r.h[at, :].astype(F32) + summed + bias).astype(BF16)
        r.h[at, :] = new
        r.normed[at, :] = layer_norm(new.astype(F32), gain, shift).astype(BF16)
        return carry

    lax.fori_loop(0, count * DRAFT // STEP, body, 0, unroll=4)

    rank = lax.axis_index("mp")
    new_writes = []
    for i in range(count):
        copy = copies.make(r.h.at[pl.ds(i * DRAFT, DRAFT)], r.new_hidden.at[order[i] % share])
        owned = order[i] // share == rank
        new_writes.append((owned, copy))
        pl.when(owned)(copy.start)
    writes = []
    for c in range(3):
        wait(got_w[c])
        linear = (dot(r.normed[...], r.w[c]) + r.b[pl.ds(c, 1), :]).astype(BF16)
        for i in range(count):
            r.o[c, i] = linear[i * DRAFT : (i + 1) * DRAFT]
            writes.append(copies.start(r.o.at[c, i], r.next_qkv.at[c, order[i]]))
    wait(*writes)
    for owned, copy in new_writes:
        pl.when(owned)(copy.wait)


def finish(sent, a, last):
    requests, _, width = a.hidden.shape
    heads_width = a.next_weight.shape[2]
    share = requests // a.n_mp
    pieces = [piece for piece, _ in sent]
    count = sum(len(piece) for piece in pieces)
    rows = count * DRAFT
    terms = len(sent[0][1])
    ins = {}
    for n in range(terms):
        for _, parts in sent:
            ins[len(ins)] = parts[n]
    ins.update(
        split_slot=a.split_slot,
        branch_bias=a.branch_bias,
        next_gain=a.next_gain,
        next_shift=a.next_shift,
        next_bias=a.next_bias,
        hidden=a.hidden,
        next_weight=a.next_weight,
    )
    aliases = {}
    if last is not None:
        ins.update(new_in=last.new_hidden, qkv_in=last.next_qkv)
        aliases = dict(new_in="new_hidden", qkv_in="next_qkv")
    outs = dict(new_hidden=(share, DRAFT, width), next_qkv=(3, requests, DRAFT, heads_width))
    scratch = dict(
        slots=SMEM(a.split_slot.shape, I32),
        bias=VMEM((1, width), F32),
        gain=VMEM((1, width), F32),
        shift=VMEM((1, width), F32),
        b=VMEM((3, heads_width), F32),
        h=VMEM((rows, width), BF16),
        t=VMEM((terms, rows, width), BF16),
        normed=VMEM((rows, width), BF16),
        w=VMEM((3, width, heads_width), BF16),
        o=VMEM((3, count, DRAFT, heads_width), BF16),
        sems=pltpu.SemaphoreType.DMA((60,)),
    )

    def kernel(names, *refs):
        finish_kernel(pieces, terms, names, *refs)

    return call(kernel, ins, outs, scratch, aliases, 60, "finish")


def local(
    hidden,
    ln_gain,
    ln_shift,
    qkv_weight,
    qkv_bias,
    out_weight,
    up_weight,
    up_bias,
    down_weight,
    branch_bias,
    next_gain,
    next_shift,
    next_weight,
    next_bias,
    key_cache,
    value_cache,
    tail_keys,
    tail_values,
    lengths,
    split_slot,
    tail_len,
    parents,
    accepted,
):
    requests = lengths.shape[0]
    width = hidden.shape[1]
    n_mp = lax.axis_size("mp")
    groups = lax.axis_size("group")
    a = SimpleNamespace(
        hidden=hidden.reshape(requests, DRAFT, width),
        ln_gain=ln_gain.reshape(1, width),
        ln_shift=ln_shift.reshape(1, width),
        qkv_weight=qkv_weight,
        qkv_bias=qkv_bias,
        out_weight=out_weight,
        up_weight=up_weight,
        up_bias=up_bias.reshape(1, -1),
        down_weight=down_weight,
        branch_bias=branch_bias.reshape(1, width),
        next_gain=next_gain.reshape(1, width),
        next_shift=next_shift.reshape(1, width),
        next_weight=next_weight,
        next_bias=next_bias,
        key_cache=key_cache,
        value_cache=value_cache,
        lengths=lengths,
        split_slot=split_slot,
        tail_len=tail_len,
        parents=parents.reshape(requests * DRAFT // PAIR, PAIR),
        accepted=accepted,
        n_mp=n_mp,
    )
    out = None
    sent = []
    for k, pieces in enumerate(CHUNKS):
        if k == 1:
            tail_keys, tail_values, _ = lax.optimization_barrier((tail_keys, tail_values, sent[0][1][0]))
            swap = [(i, i ^ 1) for i in range(groups)]
            a.far_keys, a.far_values = lax.ppermute((tail_keys, tail_values), "group", swap)
        if k >= 2:
            a.lengths, _ = lax.optimization_barrier((a.lengths, sent[k - 2][1][-1]))
        sums, out = branch(pieces, k == len(CHUNKS) - 1, a, out)
        for piece, part in zip(pieces, sums):
            if n_mp == 2:
                sent.append((piece, (part, lax.ppermute(part, "mp", [(0, 1), (1, 0)]))))
            else:
                sent.append((piece, (lax.psum(part, "mp"),)))
    a.branch_bias, _ = lax.optimization_barrier((a.branch_bias, sums))
    last = None
    for first, end in FINISHES:
        last = finish(sent[first:end], a, last)
    heads_width = qkv_weight.shape[2]
    return (
        last.new_hidden.reshape(-1, width),
        last.next_qkv.reshape(3, requests * DRAFT, heads_width),
        out.rows_out.reshape(2, -1, heads_width),
    )


def solution(mesh):
    in_specs = (
        P("group", None),
        P(),
        P(),
        P(None, None, "mp"),
        P(None, "mp"),
        P("mp", None),
        P(None, "mp"),
        P("mp"),
        P("mp", None),
        P(),
        P(),
        P(),
        P(None, None, "mp"),
        P(None, "mp"),
        P("group", None, "mp"),
        P("group", None, "mp"),
        P("group", None, "mp"),
        P("group", None, "mp"),
        P("group"),
        P("group"),
        P(),
        P("group"),
        P("group", None),
    )
    out_specs = (P(("group", "mp"), None), P(None, "group", "mp"), P(None, "group", "mp"))
    return jax.shard_map(local, mesh=mesh, in_specs=in_specs, out_specs=out_specs, check_vma=False)
```

profile of v0, /device:TPU:0, one launch (start us, length us, event | category | flops | bytes accessed | tf_op | source)
XLA Modules:
  0.0 79.6 jit_solution(2381614981069867822)
XLA Ops:
  0.6 12.3 %branch.4 = (bf16[2,8,8,512]{3,2,1,0:T(8,128)(2,1)}, bf16[3,2048,512]{2,1,0:T(8,128)(2,1)S(1)}, bf16[2048,2048]{1,0:T(8,128)(2,1)S(1)}, bf16[2048,2048]{1,0:T(8,...) custom-call(s32[8]{0:T(128)} %refs_0_.5, s32[2]{0:T(128)} %refs_2_.11, s32[32]{0:T(128)} %refs_2_.9, ...), custom_call_target="tpu_custom_call" | custom-call | tf_op jit(solution)/shard_map/branch/pallas_call | solution.py:328
  12.9 0.5 collective-permute-start.2
  13.5 0.1 collective-permute-start.3
  13.5 2.9 %collective-permute-start = (bf16[128,2048]{1,0:T(8,128)(2,1)}, bf16[128,2048]{1,0:T(8,128)(2,1)S(1)}, u32[]{:S(2)}, u32[]{:S(2)}) collective-permute-start(bf16[128,2048]{1,0:T(8,128)(2,1)} %get-tuple-element.27.refs_0_), channel_id=1, source_target_pairs={{0,1},{1,0},{2,3},{3,2},{4,5},{5,4},{6,7},{7,6},{8,9},{9,8},{10,11... | collective-permute-start | bytes 1572872 | tf_op jit(solution)/shard_map/ppermute | solution.py:597
  16.5 10.0 %branch.5 = (bf16[2,8,8,512]{3,2,1,0:T(8,128)(2,1)}, bf16[128,2048]{1,0:T(8,128)(2,1)}) custom-call(s32[8]{0:T(128)} %refs_0_.5, s32[2]{0:T(128)} %refs_2_.11, s32[32]{0:T(128)} %refs_2_.9, s32[8,8]{1,0:T(8,128)} %refs_3_.7, s32[4,128]{1,0:T(4,128)} %bitcast.43, f32[1,2048]{1,0:T(1,128)} %bitcast.22, ...), custom_call_target="tpu_custom_call", output_to_operand_aliasing={{0}: (12, {})} | custom-call | tf_op jit(solution)/shard_map/branch/pallas_call | solution.py:328
  26.5 0.1 collective-permute-start.1
  26.5 2.5 %collective-permute-done.refs_3_ = bf16[128,2048]{1,0:T(8,128)(2,1)S(1)} collective-permute-done((bf16[128,2048]{1,0:T(8,128)(2,1)}, bf16[128,2048]{1,0:T(8,128)(2,1)S(1)}, u32[]{:S(2)}, u32[]{:S(2)}) %collective-permute-start) | collective-permute-done | bytes 524320 | tf_op jit(solution)/shard_map/ppermute | solution.py:597
  29.1 0.0 copy-start
  29.1 10.0 %branch.6 = (bf16[2,8,8,512]{3,2,1,0:T(8,128)(2,1)}, bf16[128,2048]{1,0:T(8,128)(2,1)}) custom-call(s32[8]{0:T(128)} %refs_0_.5, s32[2]{0:T(128)} %refs_2_.11, s32[32]{0:T(128)} %refs_2_.9, s32[8,8]{1,0:T(8,128)} %refs_3_.7, s32[4,128]{1,0:T(4,128)} %bitcast.44, f32[1,2048]{1,0:T(1,128)} %bitcast.23, ...), custom_call_target="tpu_custom_call", output_to_operand_aliasing={{0}: (12, {})} | custom-call | tf_op jit(solution)/shard_map/branch/pallas_call | solution.py:328
  39.1 0.0 copy-done
  39.1 2.4 %collective-permute-start.6 = (bf16[128,2048]{1,0:T(8,128)(2,1)}, bf16[128,2048]{1,0:T(8,128)(2,1)S(1)}, u32[]{:S(2)}, u32[]{:S(2)}) collective-permute-start(bf16[128,2048]{1,0:T(8,128)(2,1)} %get-tuple-element.43.refs_2_), channel_id=1, source_target_pairs={{0,1},{1,0},{2,3},{3,2},{4,5},{5,4},{6,7},{7,6},{8,9},{9,8},{10,11... | collective-permute-start | bytes 1572872 | tf_op jit(solution)/shard_map/ppermute | solution.py:597
  41.6 0.0 collective-permute-done.1.refs_4_
  41.6 0.0 copy-start.1
  41.6 0.0 collective-permute-done.2.refs_12_
  41.6 0.0 collective-permute-done.3.refs_13_
  41.6 13.9 %branch.7 = (bf16[2,8,8,512]{3,2,1,0:T(8,128)(2,1)}, bf16[64,2048]{1,0:T(8,128)(2,1)}, bf16[64,2048]{1,0:T(8,128)(2,1)}) custom-call(s32[8]{0:T(128)} %refs_0_.5, s32[2]{0:T(128)} %refs_2_.11, s32[32]{0:T(128)} %refs_2_.9, s32[8,8]{1,0:T(8,128)} %refs_3_.7, s32[4,128]{1,0:T(4,128)} %bitcast.45, ...), custom_call_target="tpu_custom_call", output_to_operand_aliasing={{0}: (14, {})} | custom-call | tf_op jit(solution)/shard_map/branch/pallas_call | solution.py:328
  55.4 0.0 copy-done.1
  55.5 0.3 collective-permute-start.5
  55.8 1.8 %collective-permute-start.4 = (bf16[64,2048]{1,0:T(8,128)(2,1)}, bf16[64,2048]{1,0:T(8,128)(2,1)S(1)}, u32[]{:S(2)}, u32[]{:S(2)}) collective-permute-start(bf16[64,2048]{1,0:T(8,128)(2,1)} %get-tuple-element.40.refs_0_), channel_id=1, source_target_pairs={{0,1},{1,0},{2,3},{3,2},{4,5},{5,4},{6,7},{7,6},{8,9},{9,8},{10,11... | collective-permute-start | bytes 786440 | tf_op jit(solution)/shard_map/ppermute | solution.py:597
  57.5 0.0 collective-permute-done.6.refs_5_
  57.5 0.0 copy-start.2
  57.6 0.8 %copy-done.2 = bf16[128,2048]{1,0:T(8,128)(2,1)} copy-done((bf16[128,2048]{1,0:T(8,128)(2,1)}, bf16[128,2048]{1,0:T(8,128)(2,1)S(1)}, u32[]{:S(2)}) %copy-start.2) | copy-done | bytes 524312
  58.4 8.9 %finish.3 = (bf16[4,64,2048]{2,1,0:T(8,128)(2,1)}, bf16[3,8,64,512]{3,2,1,0:T(8,128)(2,1)}) custom-call(bf16[128,2048]{1,0:T(8,128)(2,1)} %get-tuple-element.27.refs_0_, bf16[128,2048]{1,0:T(8,128)(2,1)} %get-tuple-element.34.refs_1_, bf16[128,2048]{1,0:T(8,128)(2,1)} %get-tuple-element.43.refs_2_, bf16[128,2048]{1,0:T(8,128)(2,1)} %copy-done, ...), custom_call_target="tpu_custom_call" | custom-call | tf_op jit(solution)/shard_map/finish/pallas_call | solution.py:328
  67.3 0.0 collective-permute-done.5.refs_1_
  67.3 0.0 copy-start.4
  67.3 0.7 copy-done.4
  68.0 5.3 %finish.4 = (bf16[4,64,2048]{2,1,0:T(8,128)(2,1)}, bf16[3,8,64,512]{3,2,1,0:T(8,128)(2,1)}) custom-call(bf16[64,2048]{1,0:T(8,128)(2,1)} %get-tuple-element.41.refs_0_, bf16[64,2048]{1,0:T(8,128)(2,1)} %copy-done.4, s32[2]{0:T(128)} %refs_2_.11, f32[1,2048]{1,0:T(1,128)} %bitcast.34, ...), custom_call_target="tpu_custom_call", output_to_operand_aliasing={{0}: (9, {}), {1}: (10, {})} | custom-call | tf_op jit(solution)/shard_map/finish/pallas_call | solution.py:328
  73.3 0.0 collective-permute-done.4.refs_1_
  73.3 0.0 copy-start.3
  73.3 0.7 copy-done.3
  74.0 5.4 %finish.5 = (bf16[4,64,2048]{2,1,0:T(8,128)(2,1)}, bf16[3,8,64,512]{3,2,1,0:T(8,128)(2,1)}) custom-call(bf16[64,2048]{1,0:T(8,128)(2,1)} %get-tuple-element.40.refs_0_, bf16[64,2048]{1,0:T(8,128)(2,1)} %copy-done.3, s32[2]{0:T(128)} %refs_2_.11, f32[1,2048]{1,0:T(1,128)} %bitcast.35, ...), custom_call_target="tpu_custom_call", output_to_operand_aliasing={{0}: (9, {}), {1}: (10, {})} | custom-call | tf_op jit(solution)/shard_map/finish/pallas_call | solution.py:328
Async XLA Ops:
  12.9 28.6 %collective-permute-start.2 = (bf16[2,2048,512]{2,1,0:T(8,128)(2,1)}, bf16[2,2048,512]{2,1,0:T(8,128)(2,1)}, u32[]{:S(2)}, u32[]{:S(2)}) collective-permute-start(bf16[2,2048,512]{2,1,0:T(8,128)(2,1)} %param.39), channel_id=1, source_target_pairs={{0,2},{2,0},{4,6},{6,4},{8,10},{10,8},{12,14},{14,12},{16,18},{18,... | collective-permute-start | bytes 12582920 | tf_op jit(solution)/shard_map/ppermute | solution.py:591
  13.5 28.1 %collective-permute-start.3 = (bf16[2,2048,512]{2,1,0:T(8,128)(2,1)}, bf16[2,2048,512]{2,1,0:T(8,128)(2,1)}, u32[]{:S(2)}, u32[]{:S(2)}) collective-permute-start(bf16[2,2048,512]{2,1,0:T(8,128)(2,1)} %param.40), channel_id=1, source_target_pairs={{0,2},{2,0},{4,6},{6,4},{8,10},{10,8},{12,14},{14,12},{16,18},{18,... | collective-permute-start | bytes 12582920 | tf_op jit(solution)/shard_map/ppermute | solution.py:591
  13.5 15.5 %collective-permute-start = (bf16[128,2048]{1,0:T(8,128)(2,1)}, bf16[128,2048]{1,0:T(8,128)(2,1)S(1)}, u32[]{:S(2)}, u32[]{:S(2)}) collective-permute-start(bf16[128,2048]{1,0:T(8,128)(2,1)} %get-tuple-element.27.refs_0_), channel_id=1, source_target_pairs={{0,1},{1,0},{2,3},{3,2},{4,5},{5,4},{6,7},{7,6},{8,9},{9,8},{10,11... | collective-permute-start | bytes 1572872 | tf_op jit(solution)/shard_map/ppermute | solution.py:597
  26.5 15.1 %collective-permute-start.1 = (bf16[128,2048]{1,0:T(8,128)(2,1)}, bf16[128,2048]{1,0:T(8,128)(2,1)S(1)}, u32[]{:S(2)}, u32[]{:S(2)}) collective-permute-start(bf16[128,2048]{1,0:T(8,128)(2,1)} %get-tuple-element.34.refs_1_), channel_id=1, source_target_pairs={{0,1},{1,0},{2,3},{3,2},{4,5},{5,4},{6,7},{7,6},{8,9},{9,8},{10,11... | collective-permute-start | bytes 1572872 | tf_op jit(solution)/shard_map/ppermute | solution.py:597
  29.1 10.1 %copy-start = (bf16[128,2048]{1,0:T(8,128)(2,1)}, bf16[128,2048]{1,0:T(8,128)(2,1)S(1)}, u32[]{:S(2)}) copy-start(bf16[128,2048]{1,0:T(8,128)(2,1)S(1)} %collective-permute-done.refs_3_) | copy-start | bytes 1572868
  39.1 18.4 %collective-permute-start.6 = (bf16[128,2048]{1,0:T(8,128)(2,1)}, bf16[128,2048]{1,0:T(8,128)(2,1)S(1)}, u32[]{:S(2)}, u32[]{:S(2)}) collective-permute-start(bf16[128,2048]{1,0:T(8,128)(2,1)} %get-tuple-element.43.refs_2_), channel_id=1, source_target_pairs={{0,1},{1,0},{2,3},{3,2},{4,5},{5,4},{6,7},{7,6},{8,9},{9,8},{10,11... | collective-permute-start | bytes 1572872 | tf_op jit(solution)/shard_map/ppermute | solution.py:597
  41.6 13.9 %copy-start.1 = (bf16[128,2048]{1,0:T(8,128)(2,1)}, bf16[128,2048]{1,0:T(8,128)(2,1)S(1)}, u32[]{:S(2)}) copy-start(bf16[128,2048]{1,0:T(8,128)(2,1)S(1)} %collective-permute-done.1.refs_4_) | copy-start | bytes 1572868
  55.5 11.8 %collective-permute-start.5 = (bf16[64,2048]{1,0:T(8,128)(2,1)}, bf16[64,2048]{1,0:T(8,128)(2,1)S(1)}, u32[]{:S(2)}, u32[]{:S(2)}) collective-permute-start(bf16[64,2048]{1,0:T(8,128)(2,1)} %get-tuple-element.41.refs_0_), channel_id=1, source_target_pairs={{0,1},{1,0},{2,3},{3,2},{4,5},{5,4},{6,7},{7,6},{8,9},{9,8},{10,11... | collective-permute-start | bytes 786440 | tf_op jit(solution)/shard_map/ppermute | solution.py:597
  55.8 17.5 %collective-permute-start.4 = (bf16[64,2048]{1,0:T(8,128)(2,1)}, bf16[64,2048]{1,0:T(8,128)(2,1)S(1)}, u32[]{:S(2)}, u32[]{:S(2)}) collective-permute-start(bf16[64,2048]{1,0:T(8,128)(2,1)} %get-tuple-element.40.refs_0_), channel_id=1, source_target_pairs={{0,1},{1,0},{2,3},{3,2},{4,5},{5,4},{6,7},{7,6},{8,9},{9,8},{10,11... | collective-permute-start | bytes 786440 | tf_op jit(solution)/shard_map/ppermute | solution.py:597
  57.5 0.8 %copy-start.2 = (bf16[128,2048]{1,0:T(8,128)(2,1)}, bf16[128,2048]{1,0:T(8,128)(2,1)S(1)}, u32[]{:S(2)}) copy-start(bf16[128,2048]{1,0:T(8,128)(2,1)S(1)} %collective-permute-done.6.refs_5_) | copy-start | bytes 1572868
  67.3 0.7 copy-start.4
  73.3 0.7 copy-start.3
where the time goes:
time: 79.9 us; the launch traced here: 79.6 us
  Pallas kernels  65.8 us (82%)
  starting transfers between devices  8.1 us (10%)
  waiting for transfers between devices  2.54 us (3%)
  local copies, waits for them, and re-layouts  2.21 us (3%)
  between operations  0.93 us (1%)
    pallas_call x7, Pallas kernels, call(): pl.pallas_call(functools.partial(kernel, names), out_shape=[(VMEM if key...  65.8 us
    ppermute x5, starting transfers between devices, local(): sent.append((piece, (part, lax.ppermute(part, 'mp', [(0, 1), (1, 0)]))))  7.51 us
    ppermute x5, waiting for transfers between devices, local(): sent.append((piece, (part, lax.ppermute(part, 'mp', [(0, 1), (1, 0)]))))  2.54 us
    unnamed x10, local copies, waits for them, and re-layouts  2.21 us
  transfers between devices with their start and end apart: 7, of which 1 were waited for; matrix products, arithmetic and copies ran while one was open for 0% of the time, Pallas kernels for 60%

commit v1 on v0

--- a/solution.py
+++ b/solution.py
@@ -15,9 +15,7 @@
 PAIR = 128
 BLOCK = 512
 STEP = 16
-
-KEPT = tuple(dict(w_qkv=0, w_up=0, w_down=0, w_out=0))
-FREE = tuple(dict(far_keys=0, far_values=0)) + tuple(range(20))
+VMEM_MIB = 35
 
 epsilon = 1e-05
 very_low = -1e30
@@ -147,7 +145,7 @@
     return jnp.where(token_id == ids, 1.0, 0.0).astype(BF16)
 
 
-def branch_kernel(pieces, first, names, *refs):
+def branch_kernel(pieces, first, add_own, names, *refs):
     r = SimpleNamespace(**dict(zip(names, refs)))
     places = [place for piece in pieces for place in piece]
     count = len(places)
@@ -174,6 +172,7 @@
         copies.start(r.ln_shift, r.shift),
         copies.start(r.qkv_bias, r.b_qkv),
         copies.start(r.up_bias, r.b_up),
+        copies.start(r.branch_bias, r.bias),
     ]
     early = places[-1] < whole
     if early:
@@ -309,6 +308,9 @@
         r.act[:, cols] = gelu(dot(r.normed[...], r.w_up[:, cols]) + r.b_up[:, cols]).astype(BF16)
     if first:
         wait(got_out)
+    targets = [(r.piece_a, r.base_a)]
+    if len(pieces) > 1:
+        targets.append((r.piece_b, r.base_b))
     for n, b in enumerate(down_blocks):
         cols = pl.ds(b, BLOCK)
         summed = dot(r.att[...], r.w_out[:, cols])
@@ -316,28 +318,41 @@
             wait(got_down[n])
         r.sums[:, cols] = (summed + dot(r.act[...], r.w_down[:, cols])).astype(BF16)
         start = 0
-        for piece, target in zip(pieces, (getattr(r, n) for n in names if n.startswith("piece"))):
+        for piece, (target, base) in zip(pieces, targets):
             size = len(piece) * DRAFT
-            writes.append(copies.start(r.sums.at[pl.ds(start, size), cols], target.at[:, cols]))
+            span = pl.ds(start, size)
+            writes.append(copies.start(r.sums.at[span, cols], target.at[:, cols]))
+            for i in range(len(piece)):
+                rows_i = pl.ds(start + i * DRAFT, DRAFT)
+                kept = r.h[rows_of[start // DRAFT + i], :, cols].astype(F32) + r.bias[:, cols]
+                if add_own:
+                    kept = kept + r.sums[rows_i, cols].astype(F32)
+                r.base[rows_i, cols] = kept
+            writes.append(copies.start(r.base.at[span, cols], base.at[:, cols]))
             start += size
     wait(*writes)
 
 
-def call(kernel, ins, outs, scratch, aliases, vmem, name):
+def call(kernel, ins, outs, scratch, aliases, name):
     names = (*ins, *outs, *scratch)
+    operands = []
+    for array, space in ins.values():
+        operands.append(array if space is pl.ANY else pltpu.with_memory_space_constraint(array, space))
     results = pl.pallas_call(
         functools.partial(kernel, names),
-        out_shape=[(VMEM if key in KEPT else HBM)(shape, BF16) for key, shape in outs.items()],
-        in_specs=[
-            pl.BlockSpec(memory_space=VMEM if key in KEPT else pl.ANY if key in FREE else HBM) for key in ins
-        ],
-        out_specs=[pl.BlockSpec(memory_space=VMEM if key in KEPT else HBM) for key in outs],
+        out_shape=list(outs.values()),
+        in_specs=[pl.BlockSpec(memory_space=space) for _, space in ins.values()],
+        out_specs=[pl.BlockSpec(memory_space=ref.memory_space) for ref in outs.values()],
         scratch_shapes=list(scratch.values()),
         input_output_aliases={list(ins).index(a): list(outs).index(b) for a, b in aliases.items()},
-        compiler_params=pltpu.CompilerParams(vmem_limit_bytes=vmem * 2**20),
+        compiler_params=pltpu.CompilerParams(vmem_limit_bytes=VMEM_MIB * 2**20),
         name=name,
-    )(*(x if key in FREE else pltpu.with_memory_space_constraint(x, VMEM if key in KEPT else HBM) for key, x in ins.items()))
+    )(*operands)
     return SimpleNamespace(**dict(zip(outs, results)))
+
+
+def at(space, **arrays):
+    return {key: (array, space) for key, array in arrays.items()}
 
 
 def branch(pieces, tail, a, before):
@@ -349,7 +364,8 @@
     tails = a.split_slot.shape[0]
     count = sum(len(piece) for piece in pieces)
     rows = count * DRAFT
-    ins = dict(
+    ins = at(
+        HBM,
         lengths=a.lengths,
         split_slot=a.split_slot,
         tail_len=a.tail_len,
@@ -359,6 +375,7 @@
         ln_shift=a.ln_shift,
         qkv_bias=a.qkv_bias,
         up_bias=a.up_bias,
+        branch_bias=a.branch_bias,
         hidden=a.hidden,
         key_cache=a.key_cache,
         value_cache=a.value_cache,
@@ -373,6 +390,7 @@
         shift=VMEM((1, width), F32),
         b_qkv=VMEM((3, heads_width), F32),
         b_up=VMEM((1, units), F32),
+        bias=VMEM((1, width), F32),
         h=VMEM((count + (0 if tail else tails), DRAFT, width), BF16),
         normed=VMEM((rows, width), BF16),
         k_own=VMEM((count, cap_len, heads_width), BF16),
@@ -383,87 +401,82 @@
         att=VMEM((rows, heads_width), BF16),
         act=VMEM((rows, units), BF16),
         sums=VMEM((rows, width), BF16),
+        base=VMEM((rows, width), F32),
         picked=VMEM((2, count, acc_count, heads_width), BF16),
         sems=pltpu.SemaphoreType.DMA((100,)),
     )
-    if tail:
-        ins.update(far_keys=a.far_keys, far_values=a.far_values)
-        scratch.update(k_far=VMEM(a.far_keys.shape, BF16), v_far=VMEM(a.far_values.shape, BF16))
-    outs = dict(rows_out=(2, requests, acc_count, heads_width))
+    outs = dict(rows_out=HBM((2, requests, acc_count, heads_width), BF16))
     aliases = {}
     if before is None:
         ins.update(
-            qkv_weight=a.qkv_weight, up_weight=a.up_weight, down_weight=a.down_weight, out_weight=a.out_weight
+            at(
+                HBM,
+                qkv_weight=a.qkv_weight,
+                up_weight=a.up_weight,
+                down_weight=a.down_weight,
+                out_weight=a.out_weight,
+            )
         )
         outs.update(
-            w_qkv=a.qkv_weight.shape, w_up=a.up_weight.shape, w_down=a.down_weight.shape, w_out=a.out_weight.shape
+            w_qkv=VMEM(a.qkv_weight.shape, BF16),
+            w_up=VMEM(a.up_weight.shape, BF16),
+            w_down=VMEM(a.down_weight.shape, BF16),
+            w_out=VMEM(a.out_weight.shape, BF16),
         )
     else:
-        ins.update(
-            rows_in=before.rows_out, w_qkv=a.w_qkv, w_up=a.w_up, w_down=a.w_down, w_out=a.w_out
-        )
+        ins.update(at(HBM, rows_in=before.rows_out))
+        ins.update(at(VMEM, w_qkv=a.w_qkv, w_up=a.w_up, w_down=a.w_down, w_out=a.w_out))
         aliases = dict(rows_in="rows_out")
+    if tail:
+        ins.update(at(pl.ANY, far_keys=a.far_keys, far_values=a.far_values))
+        scratch.update(k_far=VMEM(a.far_keys.shape, BF16), v_far=VMEM(a.far_values.shape, BF16))
     sizes = [len(piece) * DRAFT for piece in pieces]
-    if len(sizes) == 1:
-        outs.update(piece_a=(sizes[0], width))
-    else:
-        outs.update(piece_a=(sizes[0], width), piece_b=(sizes[1], width))
+    outs.update(piece_a=HBM((sizes[0], width), BF16), base_a=HBM((sizes[0], width), F32))
+    if len(sizes) > 1:
+        outs.update(piece_b=HBM((sizes[1], width), BF16), base_b=HBM((sizes[1], width), F32))
 
     def kernel(names, *refs):
-        branch_kernel(pieces, before is None, names, *refs)
-
-    out = call(kernel, ins, outs, scratch, aliases, 36, "branch")
-    parts = [out.piece_a] if len(sizes) == 1 else [out.piece_a, out.piece_b]
+        branch_kernel(pieces, before is None, a.n_mp == 2, names, *refs)
+
+    out = call(kernel, ins, outs, scratch, aliases, "branch")
+    parts = [(out.piece_a, out.base_a)]
+    if len(sizes) > 1:
+        parts.append((out.piece_b, out.base_b))
     if before is None:
         a.w_qkv, a.w_up, a.w_down, a.w_out = out.w_qkv, out.w_up, out.w_down, out.w_out
     return parts, out
 
 
-def finish_kernel(pieces, terms, names, *refs):
+def finish_kernel(pieces, first, names, *refs):
     r = SimpleNamespace(**{str(name): ref for name, ref in zip(names, refs)})
-    requests, _, width = r.hidden.shape
+    given = refs[: len(pieces)]
+    kept = refs[len(pieces) : 2 * len(pieces)]
+    requests = r.next_qkv.shape[1]
     share = r.new_hidden.shape[0]
     places = [place for piece in pieces for place in piece]
     count = len(places)
     copies = Copies(r.sems)
-    wait_slots = copies.start(r.split_slot, r.slots)
-    got_terms = []
-    given = iter(refs)
-    for n in range(terms):
-        start = 0
-        for piece in pieces:
-            size = len(piece) * DRAFT
-            got_terms.append(copies.start(next(given), r.t.at[n, pl.ds(start, size)]))
-            start += size
-    got_small = [
-        copies.start(r.branch_bias, r.bias),
-        copies.start(r.next_gain, r.gain),
-        copies.start(r.next_shift, r.shift),
-        copies.start(r.next_bias, r.b),
-    ]
-    wait(wait_slots)
+    got_slots = copies.start(r.split_slot, r.slots)
+    got_w = [copies.start(r.next_weight.at[c], r.w_next.at[c]) for c in range(3)] if first else []
+    gain = r.next_gain[...]
+    shift = r.next_shift[...]
+    start = 0
+    for n, piece in enumerate(pieces):
+        size = len(piece) * DRAFT
+
+        def body(k, carry, n=n, start=start):
+            part = pl.ds(pl.multiple_of(k * STEP, STEP), STEP)
+            rows = pl.ds(pl.multiple_of(start + k * STEP, STEP), STEP)
+            new = (kept[n][part, :] + given[n][part, :].astype(F32)).astype(BF16)
+            r.h[rows, :] = new
+            r.normed[rows, :] = layer_norm(new.astype(F32), gain, shift).astype(BF16)
+            return carry
+
+        lax.fori_loop(0, size // STEP, body, 0, unroll=4)
+        start += size
+
+    wait(got_slots)
     order = [request_at(place, r.slots, requests) for place in places]
-    got_hidden = [
-        copies.start(r.hidden.at[order[i]], r.h.at[pl.ds(i * DRAFT, DRAFT)]) for i in range(count)
-    ]
-    got_w = [copies.start(r.next_weight.at[c], r.w.at[c]) for c in range(3)]
-    wait(*got_terms, *got_small, *got_hidden)
-    bias = r.bias[...]
-    gain = r.gain[...]
-    shift = r.shift[...]
-
-    def body(k, carry):
-        at = pl.ds(pl.multiple_of(k * STEP, STEP), STEP)
-        summed = r.t[0, at, :].astype(F32)
-        for n in range(1, terms):
-            summed = summed + r.t[n, at, :].astype(F32)
-        new = (r.h[at, :].astype(F32) + summed + bias).astype(BF16)
-        r.h[at, :] = new
-        r.normed[at, :] = layer_norm(new.astype(F32), gain, shift).astype(BF16)
-        return carry
-
-    lax.fori_loop(0, count * DRAFT // STEP, body, 0, unroll=4)
-
     rank = lax.axis_index("mp")
     new_writes = []
     for i in range(count):
@@ -473,8 +486,8 @@
         pl.when(owned)(copy.start)
     writes = []
     for c in range(3):
-        wait(got_w[c])
-        linear = (dot(r.normed[...], r.w[c]) + r.b[pl.ds(c, 1), :]).astype(BF16)
+        wait(*got_w[c : c + 1])
+        linear = (dot(r.normed[...], r.w_next[c]) + r.next_bias[pl.ds(c, 1), :]).astype(BF16)
         for i in range(count):
             r.o[c, i] = linear[i * DRAFT : (i + 1) * DRAFT]
             writes.append(copies.start(r.o.at[c, i], r.next_qkv.at[c, order[i]]))
@@ -487,46 +500,45 @@
     requests, _, width = a.hidden.shape
     heads_width = a.next_weight.shape[2]
     share = requests // a.n_mp
-    pieces = [piece for piece, _ in sent]
+    pieces = [piece for piece, _, _ in sent]
     count = sum(len(piece) for piece in pieces)
     rows = count * DRAFT
-    terms = len(sent[0][1])
     ins = {}
-    for n in range(terms):
-        for _, parts in sent:
-            ins[len(ins)] = parts[n]
-    ins.update(
-        split_slot=a.split_slot,
-        branch_bias=a.branch_bias,
-        next_gain=a.next_gain,
-        next_shift=a.next_shift,
-        next_bias=a.next_bias,
-        hidden=a.hidden,
-        next_weight=a.next_weight,
+    for _, given, _ in sent:
+        ins[len(ins)] = (given, VMEM)
+    for _, _, base in sent:
+        ins[len(ins)] = (base, VMEM)
+    ins.update(at(HBM, split_slot=a.split_slot))
+    ins.update(at(VMEM, next_gain=a.next_gain, next_shift=a.next_shift, next_bias=a.next_bias))
+    aliases = {}
+    kept = {}
+    if last is None:
+        ins.update(at(HBM, next_weight=a.next_weight))
+        kept = dict(w_next=VMEM(a.next_weight.shape, BF16))
+    else:
+        ins.update(at(VMEM, w_next=a.w_next))
+        ins.update(at(HBM, new_in=last.new_hidden, qkv_in=last.next_qkv))
+        aliases = dict(new_in="new_hidden", qkv_in="next_qkv")
+    outs = dict(
+        new_hidden=HBM((share, DRAFT, width), BF16),
+        next_qkv=HBM((3, requests, DRAFT, heads_width), BF16),
+        **kept,
     )
-    aliases = {}
-    if last is not None:
-        ins.update(new_in=last.new_hidden, qkv_in=last.next_qkv)
-        aliases = dict(new_in="new_hidden", qkv_in="next_qkv")
-    outs = dict(new_hidden=(share, DRAFT, width), next_qkv=(3, requests, DRAFT, heads_width))
     scratch = dict(
         slots=SMEM(a.split_slot.shape, I32),
-        bias=VMEM((1, width), F32),
-        gain=VMEM((1, width), F32),
-        shift=VMEM((1, width), F32),
-        b=VMEM((3, heads_width), F32),
         h=VMEM((rows, width), BF16),
-        t=VMEM((terms, rows, width), BF16),
         normed=VMEM((rows, width), BF16),
-        w=VMEM((3, width, heads_width), BF16),
         o=VMEM((3, count, DRAFT, heads_width), BF16),
         sems=pltpu.SemaphoreType.DMA((60,)),
     )
 
     def kernel(names, *refs):
-        finish_kernel(pieces, terms, names, *refs)
-
-    return call(kernel, ins, outs, scratch, aliases, 60, "finish")
+        finish_kernel(pieces, last is None, names, *refs)
+
+    out = call(kernel, ins, outs, scratch, aliases, "finish")
+    if last is None:
+        a.w_next = out.w_next
+    return out
 
 
 def local(
@@ -586,18 +598,17 @@
     sent = []
     for k, pieces in enumerate(CHUNKS):
         if k == 1:
-            tail_keys, tail_values, _ = lax.optimization_barrier((tail_keys, tail_values, sent[0][1][0]))
+            tail_keys, tail_values, _ = lax.optimization_barrier((tail_keys, tail_values, sent[0][2]))
             swap = [(i, i ^ 1) for i in range(groups)]
             a.far_keys, a.far_values = lax.ppermute((tail_keys, tail_values), "group", swap)
         if k >= 2:
-            a.lengths, _ = lax.optimization_barrier((a.lengths, sent[k - 2][1][-1]))
+            a.lengths, _ = lax.optimization_barrier((a.lengths, sent[k - 2][1]))
         sums, out = branch(pieces, k == len(CHUNKS) - 1, a, out)
-        for piece, part in zip(pieces, sums):
+        for piece, (part, kept) in zip(pieces, sums):
             if n_mp == 2:
-                sent.append((piece, (part, lax.ppermute(part, "mp", [(0, 1), (1, 0)]))))
+                sent.append((piece, lax.ppermute(part, "mp", [(0, 1), (1, 0)]), kept))
             else:
-                sent.append((piece, (lax.psum(part, "mp"),)))
-    a.branch_bias, _ = lax.optimization_barrier((a.branch_bias, sums))
+                sent.append((piece, lax.psum(part, "mp"), kept))
     last = None
     for first, end in FINISHES:
         last = finish(sent[first:end], a, last)

time: 79.9 us -> 71.7 us (0.90)
  Pallas kernels: 65.8 us -> 58.7 us
  local copies, waits for them, and re-layouts: 2.21 us -> 0.04 us
  waiting for transfers between devices: 2.54 us -> 3.66 us
    pallas_call x7, Pallas kernels: 65.8 us -> 58.7 us  [call(): pl.pallas_call(functools.partial(kernel, names), out_shape=list(outs.valu...]
    unnamed x10 -> x16, local copies, waits for them, and re-layouts: 2.21 us -> 0.04 us
    ppermute x5, waiting for transfers between devices: 2.54 us -> 3.66 us  [local(): sent.append((piece, lax.ppermute(part, 'mp', [(0, 1), (1, 0)]), kept))]
  transfers between devices with their start and end apart: 7 -> 7, of which waited for: 1 -> 2; matrix products, arithmetic and copies ran while one was open for 0% -> 0% of each run, Pallas kernels for 60% -> 60%
where the time goes in v1:
time: 71.7 us; the launch traced here: 71.5 us
  Pallas kernels  58.7 us (82%)
  starting transfers between devices  8.11 us (11%)
  waiting for transfers between devices  3.66 us (5%)
  between operations  0.98 us (1%)
    pallas_call x7, Pallas kernels, call(): pl.pallas_call(functools.partial(kernel, names), out_shape=list(outs.valu...  58.7 us
    ppermute x5, starting transfers between devices, local(): sent.append((piece, lax.ppermute(part, 'mp', [(0, 1), (1, 0)]), kept))  7.52 us
    ppermute x5, waiting for transfers between devices, local(): sent.append((piece, lax.ppermute(part, 'mp', [(0, 1), (1, 0)]), kept))  3.66 us
  transfers between devices with their start and end apart: 7, of which 2 were waited for; matrix products, arithmetic and copies ran while one was open for 0% of the time, Pallas kernels for 60%

profile of v1, /device:TPU:0, one launch (start us, length us, event | category | flops | bytes accessed | tf_op | source)
XLA Modules:
  0.0 71.5 jit_solution(5218260405717340324)
XLA Ops:
  0.6 12.4 %branch.4 = (bf16[2,8,8,512]{3,2,1,0:T(8,128)(2,1)}, bf16[3,2048,512]{2,1,0:T(8,128)(2,1)S(1)}, bf16[2048,2048]{1,0:T(8,128)(2,1)S(1)}, bf16[2048,2048]{1,0:T(8,...) custom-call(s32[8]{0:T(128)} %refs_0_.5, s32[2]{0:T(128)} %refs_2_.11, ...), custom_call_target="tpu_custom_call" | custom-call | tf_op jit(solution)/shard_map/branch/pallas_call | solution.py:341
  13.1 0.5 collective-permute-start.2
  13.6 0.1 collective-permute-start.3
  13.7 2.9 %collective-permute-start = (bf16[128,2048]{1,0:T(8,128)(2,1)}, bf16[128,2048]{1,0:T(8,128)(2,1)S(1)}, u32[]{:S(2)}, u32[]{:S(2)}) collective-permute-start(bf16[128,2048]{1,0:T(8,128)(2,1)} %get-tuple-element.32), channel_id=1, source_target_pairs={{0,1},{1,0},{2,3},{3,2},{4,5},{5,4},{6,7},{7,6},{8,9},{9,8},{10,11... | collective-permute-start | bytes 1572872 | tf_op jit(solution)/shard_map/ppermute | solution.py:609
  16.6 10.1 %branch.5 = (bf16[2,8,8,512]{3,2,1,0:T(8,128)(2,1)}, bf16[128,2048]{1,0:T(8,128)(2,1)}, f32[128,2048]{1,0:T(8,128)}) custom-call(s32[8]{0:T(128)} %refs_0_.5, s32[2]{0:T(128)} %refs_2_.11, s32[32]{0:T(128)} %refs_2_.9, s32[8,8]{1,0:T(8,128)} %refs_3_.7, s32[4,128]{1,0:T(4,128)} %bitcast.41, f32[1,2048]{1,0:T(1,128)} %bitcast.25, ...), custom_call_target="tpu_custom_call", output_to_operand_aliasing={{0}: (13, {})} | custom-call | tf_op jit(solution)/shard_map/branch/pallas_call | solution.py:341
  26.7 0.1 collective-permute-start.1
  26.8 2.4 %collective-permute-done.refs_0_ = bf16[128,2048]{1,0:T(8,128)(2,1)S(1)} collective-permute-done((bf16[128,2048]{1,0:T(8,128)(2,1)}, bf16[128,2048]{1,0:T(8,128)(2,1)S(1)}, u32[]{:S(2)}, u32[]{:S(2)}) %collective-permute-start) | collective-permute-done | bytes 524320 | tf_op jit(solution)/shard_map/ppermute | solution.py:609
  29.2 10.0 %branch.6 = (bf16[2,8,8,512]{3,2,1,0:T(8,128)(2,1)}, bf16[128,2048]{1,0:T(8,128)(2,1)}, f32[128,2048]{1,0:T(8,128)}) custom-call(s32[8]{0:T(128)} %refs_0_.5, s32[2]{0:T(128)} %refs_2_.11, s32[32]{0:T(128)} %refs_2_.9, s32[8,8]{1,0:T(8,128)} %refs_3_.7, s32[4,128]{1,0:T(4,128)} %bitcast.42, f32[1,2048]{1,0:T(1,128)} %bitcast.26, ...), custom_call_target="tpu_custom_call", output_to_operand_aliasing={{0}: (13, {})} | custom-call | tf_op jit(solution)/shard_map/branch/pallas_call | solution.py:341
  39.2 2.4 %collective-permute-start.5 = (bf16[128,2048]{1,0:T(8,128)(2,1)}, bf16[128,2048]{1,0:T(8,128)(2,1)S(1)}, u32[]{:S(2)}, u32[]{:S(2)}) collective-permute-start(bf16[128,2048]{1,0:T(8,128)(2,1)} %get-tuple-element.48), channel_id=1, source_target_pairs={{0,1},{1,0},{2,3},{3,2},{4,5},{5,4},{6,7},{7,6},{8,9},{9,8},{10,11... | collective-permute-start | bytes 1572872 | tf_op jit(solution)/shard_map/ppermute | solution.py:609
  41.6 0.0 collective-permute-done.1.refs_1_
  41.6 0.0 collective-permute-done.2.refs_18_
  41.6 0.0 collective-permute-done.3.refs_19_
  41.6 0.0 copy-start
  41.6 0.0 copy-start.1
  41.6 0.0 copy-start.2
  41.7 0.0 copy-start.5
  41.7 0.0 copy-start.6
  41.7 0.0 copy-start.7
  41.7 14.0 %branch.7 = (bf16[2,8,8,512]{3,2,1,0:T(8,128)(2,1)}, bf16[64,2048]{1,0:T(8,128)(2,1)}, f32[64,2048]{1,0:T(8,128)}, bf16[64,2048]{1,0:T(8,128)(2,1)}, f32[64,2048]{1,0:T(8,128)}) custom-call(s32[8]{0:T(128)} %refs_0_.5, s32[2]{0:T(128)} %refs_2_.11, s32[32]{0:T(128)} %refs_2_.9, s32[8,8]{1,0:T(8,128)} %refs_3_.7, ...), custom_call_target="tpu_custom_call", output_to_operand_aliasing={{0}: (13, {})} | custom-call | tf_op jit(solution)/shard_map/branch/pallas_call | solution.py:341
  55.7 0.4 collective-permute-start.6
  56.1 1.7 %collective-permute-start.4 = (bf16[64,2048]{1,0:T(8,128)(2,1)}, bf16[64,2048]{1,0:T(8,128)(2,1)S(1)}, u32[]{:S(2)}, u32[]{:S(2)}) collective-permute-start(bf16[64,2048]{1,0:T(8,128)(2,1)} %get-tuple-element.46), channel_id=1, source_target_pairs={{0,1},{1,0},{2,3},{3,2},{4,5},{5,4},{6,7},{7,6},{8,9},{9,8},{10,11... | collective-permute-start | bytes 786440 | tf_op jit(solution)/shard_map/ppermute | solution.py:609
  57.8 0.0 collective-permute-done.5.refs_2_
  57.8 0.0 copy-done
  57.8 0.0 copy-done.1
  57.8 0.0 copy-done.2
  57.8 0.0 copy-done.5
  57.9 0.0 copy-done.6
  57.9 0.0 copy-done.7
  57.9 0.0 copy-start.4
  57.9 6.0 %finish.3 = (bf16[4,64,2048]{2,1,0:T(8,128)(2,1)}, bf16[3,8,64,512]{3,2,1,0:T(8,128)(2,1)}, bf16[3,2048,512]{2,1,0:T(8,128)(2,1)S(1)}) custom-call(bf16[128,2048]{1,0:T(8,128)(2,1)S(1)} %collective-permute-done.refs_0_, bf16[128,2048]{1,0:T(8,128)(2,1)S(1)} %collective-permute-done.1.refs_1_, bf16[128,2048]{1,0:T(8,128)(2,1)S(1)} %collective-permute-done.5.refs_2_, ...), custom_call_target="tpu_custom_call" | custom-call | tf_op jit(solution)/shard_map/finish/pallas_call | solution.py:341
  63.9 1.2 %collective-permute-done.6.refs_0_ = bf16[64,2048]{1,0:T(8,128)(2,1)S(1)} collective-permute-done((bf16[64,2048]{1,0:T(8,128)(2,1)}, bf16[64,2048]{1,0:T(8,128)(2,1)S(1)}, u32[]{:S(2)}, u32[]{:S(2)}) %collective-permute-start.6) | collective-permute-done | bytes 262176 | tf_op jit(solution)/shard_map/ppermute | solution.py:609
  65.1 0.0 copy-done.4
  65.1 0.0 copy-start.3
  65.1 3.2 %finish.4 = (bf16[4,64,2048]{2,1,0:T(8,128)(2,1)}, bf16[3,8,64,512]{3,2,1,0:T(8,128)(2,1)}) custom-call(bf16[64,2048]{1,0:T(8,128)(2,1)S(1)} %collective-permute-done.6.refs_0_, f32[64,2048]{1,0:T(8,128)S(1)} %copy-done.4, s32[2]{0:T(128)} %refs_2_.11, f32[1,2048]{1,0:T(1,128)S(1)} %bitcast.12, ...), custom_call_target="tpu_custom_call", output_to_operand_aliasing={{0}: (7, {}), {1}: (8, {})} | custom-call | tf_op jit(solution)/shard_map/finish/pallas_call | solution.py:341
  68.3 0.0 collective-permute-done.4.refs_0_
  68.3 0.0 copy-done.3
  68.3 3.0 %finish.5 = (bf16[4,64,2048]{2,1,0:T(8,128)(2,1)}, bf16[3,8,64,512]{3,2,1,0:T(8,128)(2,1)}) custom-call(bf16[64,2048]{1,0:T(8,128)(2,1)S(1)} %collective-permute-done.4.refs_0_, f32[64,2048]{1,0:T(8,128)S(1)} %copy-done.3, s32[2]{0:T(128)} %refs_2_.11, f32[1,2048]{1,0:T(1,128)S(1)} %bitcast.13, ...), custom_call_target="tpu_custom_call", output_to_operand_aliasing={{0}: (7, {}), {1}: (8, {})} | custom-call | tf_op jit(solution)/shard_map/finish/pallas_call | solution.py:341
Async XLA Ops:
  13.1 28.5 %collective-permute-start.2 = (bf16[2,2048,512]{2,1,0:T(8,128)(2,1)}, bf16[2,2048,512]{2,1,0:T(8,128)(2,1)}, u32[]{:S(2)}, u32[]{:S(2)}) collective-permute-start(bf16[2,2048,512]{2,1,0:T(8,128)(2,1)} %param.39), channel_id=1, source_target_pairs={{0,2},{2,0},{4,6},{6,4},{8,10},{10,8},{12,14},{14,12},{16,18},{18,... | collective-permute-start | bytes 12582920 | tf_op jit(solution)/shard_map/ppermute | solution.py:603
  13.6 28.0 %collective-permute-start.3 = (bf16[2,2048,512]{2,1,0:T(8,128)(2,1)}, bf16[2,2048,512]{2,1,0:T(8,128)(2,1)}, u32[]{:S(2)}, u32[]{:S(2)}) collective-permute-start(bf16[2,2048,512]{2,1,0:T(8,128)(2,1)} %param.40), channel_id=1, source_target_pairs={{0,2},{2,0},{4,6},{6,4},{8,10},{10,8},{12,14},{14,12},{16,18},{18,... | collective-permute-start | bytes 12582920 | tf_op jit(solution)/shard_map/ppermute | solution.py:603
  13.7 15.5 %collective-permute-start = (bf16[128,2048]{1,0:T(8,128)(2,1)}, bf16[128,2048]{1,0:T(8,128)(2,1)S(1)}, u32[]{:S(2)}, u32[]{:S(2)}) collective-permute-start(bf16[128,2048]{1,0:T(8,128)(2,1)} %get-tuple-element.32), channel_id=1, source_target_pairs={{0,1},{1,0},{2,3},{3,2},{4,5},{5,4},{6,7},{7,6},{8,9},{9,8},{10,11... | collective-permute-start | bytes 1572872 | tf_op jit(solution)/shard_map/ppermute | solution.py:609
  26.7 14.9 %collective-permute-start.1 = (bf16[128,2048]{1,0:T(8,128)(2,1)}, bf16[128,2048]{1,0:T(8,128)(2,1)S(1)}, u32[]{:S(2)}, u32[]{:S(2)}) collective-permute-start(bf16[128,2048]{1,0:T(8,128)(2,1)} %get-tuple-element.39), channel_id=1, source_target_pairs={{0,1},{1,0},{2,3},{3,2},{4,5},{5,4},{6,7},{7,6},{8,9},{9,8},{10,11... | collective-permute-start | bytes 1572872 | tf_op jit(solution)/shard_map/ppermute | solution.py:609
  39.2 18.7 %collective-permute-start.5 = (bf16[128,2048]{1,0:T(8,128)(2,1)}, bf16[128,2048]{1,0:T(8,128)(2,1)S(1)}, u32[]{:S(2)}, u32[]{:S(2)}) collective-permute-start(bf16[128,2048]{1,0:T(8,128)(2,1)} %get-tuple-element.48), channel_id=1, source_target_pairs={{0,1},{1,0},{2,3},{3,2},{4,5},{5,4},{6,7},{7,6},{8,9},{9,8},{10,11... | collective-permute-start | bytes 1572872 | tf_op jit(solution)/shard_map/ppermute | solution.py:609
  41.6 16.2 %copy-start = (f32[128,2048]{1,0:T(8,128)S(1)}, f32[128,2048]{1,0:T(8,128)}, u32[]{:S(2)}) copy-start(f32[128,2048]{1,0:T(8,128)} %get-tuple-element.43.refs_3_) | copy-start | bytes 3145732
  41.6 16.2 %copy-start.1 = (f32[128,2048]{1,0:T(8,128)S(1)}, f32[128,2048]{1,0:T(8,128)}, u32[]{:S(2)}) copy-start(f32[128,2048]{1,0:T(8,128)} %get-tuple-element.49.refs_4_) | copy-start | bytes 3145732
  41.6 16.2 %copy-start.2 = (f32[128,2048]{1,0:T(8,128)S(1)}, f32[128,2048]{1,0:T(8,128)}, u32[]{:S(2)}) copy-start(f32[128,2048]{1,0:T(8,128)} %get-tuple-element.50.refs_5_) | copy-start | bytes 3145732
  41.7 16.2 %copy-start.5 = (f32[2048]{0:T(1024)S(1)}, f32[2048]{0:T(1024)}, u32[]{:S(2)}) copy-start(f32[2048]{0:T(1024)} %param.33) | copy-start | bytes 24580
  41.7 16.2 %copy-start.6 = (f32[2048]{0:T(1024)S(1)}, f32[2048]{0:T(1024)}, u32[]{:S(2)}) copy-start(f32[2048]{0:T(1024)} %param.34) | copy-start | bytes 24580
  41.7 16.2 %copy-start.7 = (f32[3,512]{1,0:T(4,128)S(1)}, f32[3,512]{1,0:T(4,128)}, u32[]{:S(2)}) copy-start(f32[3,512]{1,0:T(4,128)} %refs_5_.3) | copy-start | bytes 18436
  55.7 9.4 %collective-permute-start.6 = (bf16[64,2048]{1,0:T(8,128)(2,1)}, bf16[64,2048]{1,0:T(8,128)(2,1)S(1)}, u32[]{:S(2)}, u32[]{:S(2)}) collective-permute-start(bf16[64,2048]{1,0:T(8,128)(2,1)} %get-tuple-element.52), channel_id=1, source_target_pairs={{0,1},{1,0},{2,3},{3,2},{4,5},{5,4},{6,7},{7,6},{8,9},{9,8},{10,11... | collective-permute-start | bytes 786440 | tf_op jit(solution)/shard_map/ppermute | solution.py:609
  56.1 12.2 %collective-permute-start.4 = (bf16[64,2048]{1,0:T(8,128)(2,1)}, bf16[64,2048]{1,0:T(8,128)(2,1)S(1)}, u32[]{:S(2)}, u32[]{:S(2)}) collective-permute-start(bf16[64,2048]{1,0:T(8,128)(2,1)} %get-tuple-element.46), channel_id=1, source_target_pairs={{0,1},{1,0},{2,3},{3,2},{4,5},{5,4},{6,7},{7,6},{8,9},{9,8},{10,11... | collective-permute-start | bytes 786440 | tf_op jit(solution)/shard_map/ppermute | solution.py:609
  57.9 7.2 %copy-start.4 = (f32[64,2048]{1,0:T(8,128)S(1)}, f32[64,2048]{1,0:T(8,128)}, u32[]{:S(2)}) copy-start(f32[64,2048]{1,0:T(8,128)} %get-tuple-element.53.refs_1_) | copy-start | bytes 1572868
  65.1 3.2 %copy-start.3 = (f32[64,2048]{1,0:T(8,128)S(1)}, f32[64,2048]{1,0:T(8,128)}, u32[]{:S(2)}) copy-start(f32[64,2048]{1,0:T(8,128)} %get-tuple-element.47.refs_1_) | copy-start | bytes 1572868

commit v2 on v1

--- a/solution.py
+++ b/solution.py
@@ -27,8 +27,8 @@
 F32 = jnp.float32
 BF16 = jnp.bfloat16
 
-CHUNKS = (((0, 1),), ((2, 3),), ((4, 5),), ((6,), (7,)))
-FINISHES = ((0, 3), (3, 4), (4, 5))
+CHUNKS = (((0, 1),), ((2, 3, 4),), ((5, 6),), ((7,),))
+FINISHES = ((0, 2), (2, 3), (3, 4))
 
 
 def dot(a, b):
@@ -207,18 +207,19 @@
             for b in down_blocks
         ]
     if places[-1] >= whole:
+        held = [place - whole for place in places if place >= whole]
         got_far = [
-            (copies.start(r.far_keys.at[t], r.k_far.at[t]), copies.start(r.far_values.at[t], r.v_far.at[t]))
-            for t in range(tails)
+            (copies.start(r.far_keys.at[t], r.k_far.at[n]), copies.start(r.far_values.at[t], r.v_far.at[n]))
+            for n, t in enumerate(held)
         ]
 
     wait(*got_small)
     reach = []
     tables = []
     for i in range(0, count, 2):
-        both = ancestor_pair(r.tree, order[i], order[i + 1])
+        both = ancestor_pair(r.tree, order[i], order[min(i + 1, count - 1)])
         depth = jnp.sum(both, axis=1, keepdims=True) - 1.0
-        for k in (0, 1):
+        for k in range(min(2, count - i)):
             span = slice(k * DRAFT, (k + 1) * DRAFT)
             reach.append(both[span, span])
             base = r.own_len[order[i + k]].astype(F32)
@@ -259,7 +260,8 @@
         wait(*got_own[i])
         t = places[i] - whole
         if t >= 0:
-            wait(*got_far[t])
+            n_far = held.index(t)
+            wait(*got_far[n_far])
         span = pl.ds(i * DRAFT, DRAFT)
         key_id = lax.broadcasted_iota(I32, (1, cap_len), 1)
         own_bias = jnp.where(key_id < r.own_len[order[i]], 0.0, very_low)
@@ -288,12 +290,12 @@
                     part = slice(start, start + BLOCK)
                     far_id = lax.broadcasted_iota(I32, (1, BLOCK), 1) + start
                     far_bias = jnp.where(far_id < far_len, 0.0, very_low)
-                    far = dot_nt(query, r.k_far[t, part, cols]) + far_bias
+                    far = dot_nt(query, r.k_far[n_far, part, cols]) + far_bias
                     peak = jnp.maximum(top, jnp.max(far, axis=1, keepdims=True))
                     keep = jnp.exp(top - peak)
                     far = jnp.exp(far - peak)
                     total = total * keep + jnp.sum(far, axis=1, keepdims=True)
-                    mixed = mixed * keep + dot(far.astype(BF16), r.v_far[t, part, cols])
+                    mixed = mixed * keep + dot(far.astype(BF16), r.v_far[n_far, part, cols])
                     top = peak
             mixed = mixed * (1.0 / total)
             joined = jnp.zeros((DRAFT, group), F32)
@@ -355,7 +357,7 @@
     return {key: (array, space) for key, array in arrays.items()}
 
 
-def branch(pieces, tail, a, before):
+def branch(pieces, a, before):
     requests, _, width = a.hidden.shape
     heads_width = a.qkv_weight.shape[2]
     units = a.up_weight.shape[1]
@@ -364,6 +366,7 @@
     tails = a.split_slot.shape[0]
     count = sum(len(piece) for piece in pieces)
     rows = count * DRAFT
+    tail = sum(place >= requests - tails for piece in pieces for place in piece)
     ins = at(
         HBM,
         lengths=a.lengths,
@@ -429,7 +432,8 @@
         aliases = dict(rows_in="rows_out")
     if tail:
         ins.update(at(pl.ANY, far_keys=a.far_keys, far_values=a.far_values))
-        scratch.update(k_far=VMEM(a.far_keys.shape, BF16), v_far=VMEM(a.far_values.shape, BF16))
+        far_shape = (tail, *a.far_keys.shape[1:])
+        scratch.update(k_far=VMEM(far_shape, BF16), v_far=VMEM(far_shape, BF16))
     sizes = [len(piece) * DRAFT for piece in pieces]
     outs.update(piece_a=HBM((sizes[0], width), BF16), base_a=HBM((sizes[0], width), F32))
     if len(sizes) > 1:
@@ -601,9 +605,9 @@
             tail_keys, tail_values, _ = lax.optimization_barrier((tail_keys, tail_values, sent[0][2]))
             swap = [(i, i ^ 1) for i in range(groups)]
             a.far_keys, a.far_values = lax.ppermute((tail_keys, tail_values), "group", swap)
-        if k >= 2:
+        if k == 2:
             a.lengths, _ = lax.optimization_barrier((a.lengths, sent[k - 2][1]))
-        sums, out = branch(pieces, k == len(CHUNKS) - 1, a, out)
+        sums, out = branch(pieces, a, out)
         for piece, (part, kept) in zip(pieces, sums):
             if n_mp == 2:
                 sent.append((piece, lax.ppermute(part, "mp", [(0, 1), (1, 0)]), kept))

time: 71.7 us -> 69.7 us (0.972)
  starting transfers between devices: 8.11 us -> 5.74 us
  Pallas kernels: 58.7 us -> 60.1 us
  waiting for transfers between devices: 3.66 us -> 2.61 us
    ppermute x5 -> x4, starting transfers between devices: 7.52 us -> 5.14 us  [local(): sent.append((piece, lax.ppermute(part, 'mp', [(0, 1), (1, 0)]), kept))]
    pallas_call x7, Pallas kernels: 58.7 us -> 60.1 us  [call(): pl.pallas_call(functools.partial(kernel, names), out_shape=list(outs.valu...]
    ppermute x5 -> x4, waiting for transfers between devices: 3.66 us -> 2.61 us  [local(): sent.append((piece, lax.ppermute(part, 'mp', [(0, 1), (1, 0)]), kept))]
  transfers between devices with their start and end apart: 7 -> 6, of which waited for: 2 -> 2; matrix products, arithmetic and copies ran while one was open for 0% -> 0% of each run, Pallas kernels for 60% -> 64%
where the time goes in v2:
time: 69.7 us; the launch traced here: 69.4 us
  Pallas kernels  60.1 us (86%)
  starting transfers between devices  5.74 us (8%)
  waiting for transfers between devices  2.61 us (4%)
  between operations  0.94 us (1%)
    pallas_call x7, Pallas kernels, call(): pl.pallas_call(functools.partial(kernel, names), out_shape=list(outs.valu...  60.1 us
    ppermute x4, starting transfers between devices, local(): sent.append((piece, lax.ppermute(part, 'mp', [(0, 1), (1, 0)]), kept))  5.14 us
    ppermute x4, waiting for transfers between devices, local(): sent.append((piece, lax.ppermute(part, 'mp', [(0, 1), (1, 0)]), kept))  2.61 us
  transfers between devices with their start and end apart: 6, of which 2 were waited for; matrix products, arithmetic and copies ran while one was open for 0% of the time, Pallas kernels for 64%

profile of v2, /device:TPU:0, one launch (start us, length us, event | category | flops | bytes accessed | tf_op | source)
XLA Modules:
  0.0 69.4 jit_solution(13114145215642554901)
XLA Ops:
  0.6 12.4 %branch.4 = (bf16[2,8,8,512]{3,2,1,0:T(8,128)(2,1)}, bf16[3,2048,512]{2,1,0:T(8,128)(2,1)S(1)}, bf16[2048,2048]{1,0:T(8,128)(2,1)S(1)}, bf16[2048,2048]{1,0:T(8,...) custom-call(s32[8]{0:T(128)} %refs_0_.5, s32[2]{0:T(128)} %refs_2_.11, ...), custom_call_target="tpu_custom_call" | custom-call | tf_op jit(solution)/shard_map/branch/pallas_call | solution.py:343
  13.1 0.5 collective-permute-start.1
  13.6 0.1 collective-permute-start.2
  13.7 2.9 %collective-permute-start = (bf16[128,2048]{1,0:T(8,128)(2,1)}, bf16[128,2048]{1,0:T(8,128)(2,1)S(1)}, u32[]{:S(2)}, u32[]{:S(2)}) collective-permute-start(bf16[128,2048]{1,0:T(8,128)(2,1)} %get-tuple-element.29), channel_id=1, source_target_pairs={{0,1},{1,0},{2,3},{3,2},{4,5},{5,4},{6,7},{7,6},{8,9},{9,8},{10,11... | collective-permute-start | bytes 1572872 | tf_op jit(solution)/shard_map/ppermute | solution.py:613
  16.6 13.3 %branch.5 = (bf16[2,8,8,512]{3,2,1,0:T(8,128)(2,1)}, bf16[192,2048]{1,0:T(8,128)(2,1)}, f32[192,2048]{1,0:T(8,128)}) custom-call(s32[8]{0:T(128)} %refs_0_.5, s32[2]{0:T(128)} %refs_2_.11, s32[32]{0:T(128)} %refs_2_.9, s32[8,8]{1,0:T(8,128)} %refs_3_.7, s32[4,128]{1,0:T(4,128)} %bitcast.41, f32[1,2048]{1,0:T(1,128)} %bitcast.25, ...), custom_call_target="tpu_custom_call", output_to_operand_aliasing={{0}: (13, {})} | custom-call | tf_op jit(solution)/shard_map/branch/pallas_call | solution.py:343
  29.9 0.1 collective-permute-start.4
  29.9 0.0 collective-permute-done.refs_0_
  30.0 0.0 collective-permute-done.1.refs_18_
  30.0 0.0 collective-permute-done.2.refs_19_
  30.0 12.0 %branch.6 = (bf16[2,8,8,512]{3,2,1,0:T(8,128)(2,1)}, bf16[128,2048]{1,0:T(8,128)(2,1)}, f32[128,2048]{1,0:T(8,128)}) custom-call(s32[8]{0:T(128)} %refs_0_.5, s32[2]{0:T(128)} %refs_2_.11, s32[32]{0:T(128)} %refs_2_.9, s32[8,8]{1,0:T(8,128)} %refs_3_.7, s32[4,128]{1,0:T(4,128)} %bitcast.42, f32[1,2048]{1,0:T(1,128)} %bitcast.26, ...), custom_call_target="tpu_custom_call", output_to_operand_aliasing={{0}: (13, {})} | custom-call | tf_op jit(solution)/shard_map/branch/pallas_call | solution.py:343
  42.0 2.1 %collective-permute-start.5 = (bf16[128,2048]{1,0:T(8,128)(2,1)}, bf16[128,2048]{1,0:T(8,128)(2,1)S(1)}, u32[]{:S(2)}, u32[]{:S(2)}) collective-permute-start(bf16[128,2048]{1,0:T(8,128)(2,1)} %get-tuple-element.46), channel_id=1, source_target_pairs={{0,1},{1,0},{2,3},{3,2},{4,5},{5,4},{6,7},{7,6},{8,9},{9,8},{10,11... | collective-permute-start | bytes 1572872 | tf_op jit(solution)/shard_map/ppermute | solution.py:613
  44.1 0.0 copy-start
  44.1 0.0 copy-start.1
  44.1 0.0 copy-start.4
  44.1 0.0 copy-start.5
  44.1 0.0 copy-start.6
  44.1 11.0 %branch.7 = (bf16[2,8,8,512]{3,2,1,0:T(8,128)(2,1)}, bf16[64,2048]{1,0:T(8,128)(2,1)}, f32[64,2048]{1,0:T(8,128)}) custom-call(s32[8]{0:T(128)} %refs_0_.5, s32[2]{0:T(128)} %refs_2_.11, s32[32]{0:T(128)} %refs_2_.9, s32[8,8]{1,0:T(8,128)} %refs_3_.7, s32[4,128]{1,0:T(4,128)} %bitcast.43, f32[1,2048]{1,0:T(1,128)} %bitcast.27, ...), custom_call_target="tpu_custom_call", output_to_operand_aliasing={{0}: (13, {})} | custom-call | tf_op jit(solution)/shard_map/branch/pallas_call | solution.py:343
  55.1 0.1 collective-permute-start.3
  55.2 0.0 collective-permute-done.4.refs_1_
  55.2 0.0 copy-done
  55.2 0.0 copy-done.1
  55.2 0.0 copy-done.4
  55.2 0.0 copy-done.5
  55.2 0.0 copy-done.6
  55.3 0.0 copy-start.2
  55.3 5.4 %finish.3 = (bf16[4,64,2048]{2,1,0:T(8,128)(2,1)}, bf16[3,8,64,512]{3,2,1,0:T(8,128)(2,1)}, bf16[3,2048,512]{2,1,0:T(8,128)(2,1)S(1)}) custom-call(bf16[128,2048]{1,0:T(8,128)(2,1)S(1)} %collective-permute-done.refs_0_, bf16[192,2048]{1,0:T(8,128)(2,1)S(1)} %collective-permute-done.4.refs_1_, f32[128,2048]{1,0:T(8,128)S(1)} %copy-done.1, ...), custom_call_target="tpu_custom_call" | custom-call | tf_op jit(solution)/shard_map/finish/pallas_call | solution.py:343
  60.7 1.1 %collective-permute-done.5.refs_0_ = bf16[128,2048]{1,0:T(8,128)(2,1)S(1)} collective-permute-done((bf16[128,2048]{1,0:T(8,128)(2,1)}, bf16[128,2048]{1,0:T(8,128)(2,1)S(1)}, u32[]{:S(2)}, u32[]{:S(2)}) %collective-permute-start.5) | collective-permute-done | bytes 524320 | tf_op jit(solution)/shard_map/ppermute | solution.py:613
  61.8 0.0 copy-done.2
  61.8 0.0 copy-start.3
  61.8 3.0 %finish.4 = (bf16[4,64,2048]{2,1,0:T(8,128)(2,1)}, bf16[3,8,64,512]{3,2,1,0:T(8,128)(2,1)}) custom-call(bf16[128,2048]{1,0:T(8,128)(2,1)S(1)} %collective-permute-done.5.refs_0_, f32[128,2048]{1,0:T(8,128)S(1)} %copy-done.2, s32[2]{0:T(128)} %refs_2_.11, f32[1,2048]{1,0:T(1,128)S(1)} %bitcast.12, ...), custom_call_target="tpu_custom_call", output_to_operand_aliasing={{0}: (7, {}), {1}: (8, {})} | custom-call | tf_op jit(solution)/shard_map/finish/pallas_call | solution.py:343
  64.8 1.5 %collective-permute-done.3.refs_0_ = bf16[64,2048]{1,0:T(8,128)(2,1)S(1)} collective-permute-done((bf16[64,2048]{1,0:T(8,128)(2,1)}, bf16[64,2048]{1,0:T(8,128)(2,1)S(1)}, u32[]{:S(2)}, u32[]{:S(2)}) %collective-permute-start.3) | collective-permute-done | bytes 262176 | tf_op jit(solution)/shard_map/ppermute | solution.py:613
  66.2 0.0 copy-done.3
  66.2 3.0 %finish.5 = (bf16[4,64,2048]{2,1,0:T(8,128)(2,1)}, bf16[3,8,64,512]{3,2,1,0:T(8,128)(2,1)}) custom-call(bf16[64,2048]{1,0:T(8,128)(2,1)S(1)} %collective-permute-done.3.refs_0_, f32[64,2048]{1,0:T(8,128)S(1)} %copy-done.3, s32[2]{0:T(128)} %refs_2_.11, f32[1,2048]{1,0:T(1,128)S(1)} %bitcast.13, ...), custom_call_target="tpu_custom_call", output_to_operand_aliasing={{0}: (7, {}), {1}: (8, {})} | custom-call | tf_op jit(solution)/shard_map/finish/pallas_call | solution.py:343
Async XLA Ops:
  13.1 16.9 %collective-permute-start.1 = (bf16[2,2048,512]{2,1,0:T(8,128)(2,1)}, bf16[2,2048,512]{2,1,0:T(8,128)(2,1)}, u32[]{:S(2)}, u32[]{:S(2)}) collective-permute-start(bf16[2,2048,512]{2,1,0:T(8,128)(2,1)} %param.39), channel_id=1, source_target_pairs={{0,2},{2,0},{4,6},{6,4},{8,10},{10,8},{12,14},{14,12},{16,18},{18,... | collective-permute-start | bytes 12582920 | tf_op jit(solution)/shard_map/ppermute | solution.py:607
  13.6 16.4 %collective-permute-start.2 = (bf16[2,2048,512]{2,1,0:T(8,128)(2,1)}, bf16[2,2048,512]{2,1,0:T(8,128)(2,1)}, u32[]{:S(2)}, u32[]{:S(2)}) collective-permute-start(bf16[2,2048,512]{2,1,0:T(8,128)(2,1)} %param.40), channel_id=1, source_target_pairs={{0,2},{2,0},{4,6},{6,4},{8,10},{10,8},{12,14},{14,12},{16,18},{18,... | collective-permute-start | bytes 12582920 | tf_op jit(solution)/shard_map/ppermute | solution.py:607
  13.7 16.3 %collective-permute-start = (bf16[128,2048]{1,0:T(8,128)(2,1)}, bf16[128,2048]{1,0:T(8,128)(2,1)S(1)}, u32[]{:S(2)}, u32[]{:S(2)}) collective-permute-start(bf16[128,2048]{1,0:T(8,128)(2,1)} %get-tuple-element.29), channel_id=1, source_target_pairs={{0,1},{1,0},{2,3},{3,2},{4,5},{5,4},{6,7},{7,6},{8,9},{9,8},{10,11... | collective-permute-start | bytes 1572872 | tf_op jit(solution)/shard_map/ppermute | solution.py:613
  29.9 25.4 %collective-permute-start.4 = (bf16[192,2048]{1,0:T(8,128)(2,1)}, bf16[192,2048]{1,0:T(8,128)(2,1)S(1)}, u32[]{:S(2)}, u32[]{:S(2)}) collective-permute-start(bf16[192,2048]{1,0:T(8,128)(2,1)} %get-tuple-element.43), channel_id=1, source_target_pairs={{0,1},{1,0},{2,3},{3,2},{4,5},{5,4},{6,7},{7,6},{8,9},{9,8},{10,11... | collective-permute-start | bytes 2359304 | tf_op jit(solution)/shard_map/ppermute | solution.py:613
  42.0 19.8 %collective-permute-start.5 = (bf16[128,2048]{1,0:T(8,128)(2,1)}, bf16[128,2048]{1,0:T(8,128)(2,1)S(1)}, u32[]{:S(2)}, u32[]{:S(2)}) collective-permute-start(bf16[128,2048]{1,0:T(8,128)(2,1)} %get-tuple-element.46), channel_id=1, source_target_pairs={{0,1},{1,0},{2,3},{3,2},{4,5},{5,4},{6,7},{7,6},{8,9},{9,8},{10,11... | collective-permute-start | bytes 1572872 | tf_op jit(solution)/shard_map/ppermute | solution.py:613
  44.1 11.1 %copy-start = (f32[192,2048]{1,0:T(8,128)S(1)}, f32[192,2048]{1,0:T(8,128)}, u32[]{:S(2)}) copy-start(f32[192,2048]{1,0:T(8,128)} %get-tuple-element.44.refs_3_) | copy-start | bytes 4718596
  44.1 11.1 %copy-start.1 = (f32[128,2048]{1,0:T(8,128)S(1)}, f32[128,2048]{1,0:T(8,128)}, u32[]{:S(2)}) copy-start(f32[128,2048]{1,0:T(8,128)} %get-tuple-element.37.refs_2_) | copy-start | bytes 3145732
  44.1 11.2 %copy-start.4 = (f32[2048]{0:T(1024)S(1)}, f32[2048]{0:T(1024)}, u32[]{:S(2)}) copy-start(f32[2048]{0:T(1024)} %param.33) | copy-start | bytes 24580
  44.1 11.2 %copy-start.5 = (f32[2048]{0:T(1024)S(1)}, f32[2048]{0:T(1024)}, u32[]{:S(2)}) copy-start(f32[2048]{0:T(1024)} %param.34) | copy-start | bytes 24580
  44.1 11.2 %copy-start.6 = (f32[3,512]{1,0:T(4,128)S(1)}, f32[3,512]{1,0:T(4,128)}, u32[]{:S(2)}) copy-start(f32[3,512]{1,0:T(4,128)} %refs_5_.3) | copy-start | bytes 18436
  55.1 11.1 %collective-permute-start.3 = (bf16[64,2048]{1,0:T(8,128)(2,1)}, bf16[64,2048]{1,0:T(8,128)(2,1)S(1)}, u32[]{:S(2)}, u32[]{:S(2)}) collective-permute-start(bf16[64,2048]{1,0:T(8,128)(2,1)} %get-tuple-element.41), channel_id=1, source_target_pairs={{0,1},{1,0},{2,3},{3,2},{4,5},{5,4},{6,7},{7,6},{8,9},{9,8},{10,11... | collective-permute-start | bytes 786440 | tf_op jit(solution)/shard_map/ppermute | solution.py:613
  55.3 6.6 %copy-start.2 = (f32[128,2048]{1,0:T(8,128)S(1)}, f32[128,2048]{1,0:T(8,128)}, u32[]{:S(2)}) copy-start(f32[128,2048]{1,0:T(8,128)} %get-tuple-element.47.refs_1_) | copy-start | bytes 3145732
  61.8 4.4 %copy-start.3 = (f32[64,2048]{1,0:T(8,128)S(1)}, f32[64,2048]{1,0:T(8,128)}, u32[]{:S(2)}) copy-start(f32[64,2048]{1,0:T(8,128)} %get-tuple-element.42.refs_1_) | copy-start | bytes 1572868

commit v3 on v2

--- a/solution.py
+++ b/solution.py
@@ -14,6 +14,7 @@
 DRAFT = 64
 PAIR = 128
 BLOCK = 512
+FAR_BLOCK = 1024
 STEP = 16
 VMEM_MIB = 35
 
@@ -286,9 +287,9 @@
             if t >= 0:
                 far_cap = r.k_far.shape[1]
                 far_len = r.all_len[far_base + t]
-                for start in range(0, far_cap, BLOCK):
-                    part = slice(start, start + BLOCK)
-                    far_id = lax.broadcasted_iota(I32, (1, BLOCK), 1) + start
+                for start in range(0, far_cap, FAR_BLOCK):
+                    part = slice(start, start + FAR_BLOCK)
+                    far_id = lax.broadcasted_iota(I32, (1, FAR_BLOCK), 1) + start
                     far_bias = jnp.where(far_id < far_len, 0.0, very_low)
                     far = dot_nt(query, r.k_far[n_far, part, cols]) + far_bias
                     peak = jnp.maximum(top, jnp.max(far, axis=1, keepdims=True))

time: 69.7 us -> 69.7 us (level)
  transfers between devices with their start and end apart: 6 -> 6, of which waited for: 2 -> 2; matrix products, arithmetic and copies ran while one was open for 0% -> 0% of each run, Pallas kernels for 64% -> 65%
where the time goes in v3:
time: 69.7 us; the launch traced here: 69.4 us
  Pallas kernels  60.3 us (87%)
  starting transfers between devices  5.74 us (8%)
  waiting for transfers between devices  2.46 us (4%)
  between operations  0.94 us (1%)
    pallas_call x7, Pallas kernels, call(): pl.pallas_call(functools.partial(kernel, names), out_shape=list(outs.valu...  60.3 us
    ppermute x4, starting transfers between devices, local(): sent.append((piece, lax.ppermute(part, 'mp', [(0, 1), (1, 0)]), kept))  5.15 us
    ppermute x4, waiting for transfers between devices, local(): sent.append((piece, lax.ppermute(part, 'mp', [(0, 1), (1, 0)]), kept))  2.46 us
  transfers between devices with their start and end apart: 6, of which 2 were waited for; matrix products, arithmetic and copies ran while one was open for 0% of the time, Pallas kernels for 65%

profile of v3, /device:TPU:0, one launch (start us, length us, event | category | flops | bytes accessed | tf_op | source)
XLA Modules:
  0.0 69.4 jit_solution(16312273389840610137)
XLA Ops:
  0.6 12.4 %branch.4 = (bf16[2,8,8,512]{3,2,1,0:T(8,128)(2,1)}, bf16[3,2048,512]{2,1,0:T(8,128)(2,1)S(1)}, bf16[2048,2048]{1,0:T(8,128)(2,1)S(1)}, bf16[2048,2048]{1,0:T(8,...) custom-call(s32[8]{0:T(128)} %refs_0_.5, s32[2]{0:T(128)} %refs_2_.11, ...), custom_call_target="tpu_custom_call" | custom-call | tf_op jit(solution)/shard_map/branch/pallas_call | solution.py:344
  13.1 0.5 collective-permute-start.1
  13.6 0.1 collective-permute-start.2
  13.7 2.9 %collective-permute-start = (bf16[128,2048]{1,0:T(8,128)(2,1)}, bf16[128,2048]{1,0:T(8,128)(2,1)S(1)}, u32[]{:S(2)}, u32[]{:S(2)}) collective-permute-start(bf16[128,2048]{1,0:T(8,128)(2,1)} %get-tuple-element.29), channel_id=1, source_target_pairs={{0,1},{1,0},{2,3},{3,2},{4,5},{5,4},{6,7},{7,6},{8,9},{9,8},{10,11... | collective-permute-start | bytes 1572872 | tf_op jit(solution)/shard_map/ppermute | solution.py:614
  16.6 13.3 %branch.5 = (bf16[2,8,8,512]{3,2,1,0:T(8,128)(2,1)}, bf16[192,2048]{1,0:T(8,128)(2,1)}, f32[192,2048]{1,0:T(8,128)}) custom-call(s32[8]{0:T(128)} %refs_0_.5, s32[2]{0:T(128)} %refs_2_.11, s32[32]{0:T(128)} %refs_2_.9, s32[8,8]{1,0:T(8,128)} %refs_3_.7, s32[4,128]{1,0:T(4,128)} %bitcast.41, f32[1,2048]{1,0:T(1,128)} %bitcast.25, ...), custom_call_target="tpu_custom_call", output_to_operand_aliasing={{0}: (13, {})} | custom-call | tf_op jit(solution)/shard_map/branch/pallas_call | solution.py:344
  29.9 0.1 collective-permute-start.4
  29.9 0.0 collective-permute-done.refs_0_
  30.0 0.0 collective-permute-done.1.refs_18_
  30.0 0.0 collective-permute-done.2.refs_19_
  30.0 12.0 %branch.6 = (bf16[2,8,8,512]{3,2,1,0:T(8,128)(2,1)}, bf16[128,2048]{1,0:T(8,128)(2,1)}, f32[128,2048]{1,0:T(8,128)}) custom-call(s32[8]{0:T(128)} %refs_0_.5, s32[2]{0:T(128)} %refs_2_.11, s32[32]{0:T(128)} %refs_2_.9, s32[8,8]{1,0:T(8,128)} %refs_3_.7, s32[4,128]{1,0:T(4,128)} %bitcast.42, f32[1,2048]{1,0:T(1,128)} %bitcast.26, ...), custom_call_target="tpu_custom_call", output_to_operand_aliasing={{0}: (13, {})} | custom-call | tf_op jit(solution)/shard_map/branch/pallas_call | solution.py:344
  42.0 2.1 %collective-permute-start.5 = (bf16[128,2048]{1,0:T(8,128)(2,1)}, bf16[128,2048]{1,0:T(8,128)(2,1)S(1)}, u32[]{:S(2)}, u32[]{:S(2)}) collective-permute-start(bf16[128,2048]{1,0:T(8,128)(2,1)} %get-tuple-element.46), channel_id=1, source_target_pairs={{0,1},{1,0},{2,3},{3,2},{4,5},{5,4},{6,7},{7,6},{8,9},{9,8},{10,11... | collective-permute-start | bytes 1572872 | tf_op jit(solution)/shard_map/ppermute | solution.py:614
  44.0 0.0 copy-start
  44.0 0.0 copy-start.1
  44.0 0.0 copy-start.4
  44.0 0.0 copy-start.5
  44.0 0.0 copy-start.6
  44.0 11.2 %branch.7 = (bf16[2,8,8,512]{3,2,1,0:T(8,128)(2,1)}, bf16[64,2048]{1,0:T(8,128)(2,1)}, f32[64,2048]{1,0:T(8,128)}) custom-call(s32[8]{0:T(128)} %refs_0_.5, s32[2]{0:T(128)} %refs_2_.11, s32[32]{0:T(128)} %refs_2_.9, s32[8,8]{1,0:T(8,128)} %refs_3_.7, s32[4,128]{1,0:T(4,128)} %bitcast.43, f32[1,2048]{1,0:T(1,128)} %bitcast.27, ...), custom_call_target="tpu_custom_call", output_to_operand_aliasing={{0}: (13, {})} | custom-call | tf_op jit(solution)/shard_map/branch/pallas_call | solution.py:344
  55.2 0.1 collective-permute-start.3
  55.4 0.0 collective-permute-done.4.refs_1_
  55.4 0.0 copy-done
  55.4 0.0 copy-done.1
  55.4 0.0 copy-done.4
  55.4 0.0 copy-done.5
  55.4 0.0 copy-done.6
  55.4 0.0 copy-start.2
  55.4 5.4 %finish.3 = (bf16[4,64,2048]{2,1,0:T(8,128)(2,1)}, bf16[3,8,64,512]{3,2,1,0:T(8,128)(2,1)}, bf16[3,2048,512]{2,1,0:T(8,128)(2,1)S(1)}) custom-call(bf16[128,2048]{1,0:T(8,128)(2,1)S(1)} %collective-permute-done.refs_0_, bf16[192,2048]{1,0:T(8,128)(2,1)S(1)} %collective-permute-done.4.refs_1_, f32[128,2048]{1,0:T(8,128)S(1)} %copy-done.1, ...), custom_call_target="tpu_custom_call" | custom-call | tf_op jit(solution)/shard_map/finish/pallas_call | solution.py:344
  60.8 1.0 %collective-permute-done.5.refs_0_ = bf16[128,2048]{1,0:T(8,128)(2,1)S(1)} collective-permute-done((bf16[128,2048]{1,0:T(8,128)(2,1)}, bf16[128,2048]{1,0:T(8,128)(2,1)S(1)}, u32[]{:S(2)}, u32[]{:S(2)}) %collective-permute-start.5) | collective-permute-done | bytes 524320 | tf_op jit(solution)/shard_map/ppermute | solution.py:614
  61.8 0.0 copy-done.2
  61.8 0.0 copy-start.3
  61.8 3.0 %finish.4 = (bf16[4,64,2048]{2,1,0:T(8,128)(2,1)}, bf16[3,8,64,512]{3,2,1,0:T(8,128)(2,1)}) custom-call(bf16[128,2048]{1,0:T(8,128)(2,1)S(1)} %collective-permute-done.5.refs_0_, f32[128,2048]{1,0:T(8,128)S(1)} %copy-done.2, s32[2]{0:T(128)} %refs_2_.11, f32[1,2048]{1,0:T(1,128)S(1)} %bitcast.12, ...), custom_call_target="tpu_custom_call", output_to_operand_aliasing={{0}: (7, {}), {1}: (8, {})} | custom-call | tf_op jit(solution)/shard_map/finish/pallas_call | solution.py:344
  64.8 1.5 %collective-permute-done.3.refs_0_ = bf16[64,2048]{1,0:T(8,128)(2,1)S(1)} collective-permute-done((bf16[64,2048]{1,0:T(8,128)(2,1)}, bf16[64,2048]{1,0:T(8,128)(2,1)S(1)}, u32[]{:S(2)}, u32[]{:S(2)}) %collective-permute-start.3) | collective-permute-done | bytes 262176 | tf_op jit(solution)/shard_map/ppermute | solution.py:614
  66.2 0.0 copy-done.3
  66.2 3.0 %finish.5 = (bf16[4,64,2048]{2,1,0:T(8,128)(2,1)}, bf16[3,8,64,512]{3,2,1,0:T(8,128)(2,1)}) custom-call(bf16[64,2048]{1,0:T(8,128)(2,1)S(1)} %collective-permute-done.3.refs_0_, f32[64,2048]{1,0:T(8,128)S(1)} %copy-done.3, s32[2]{0:T(128)} %refs_2_.11, f32[1,2048]{1,0:T(1,128)S(1)} %bitcast.13, ...), custom_call_target="tpu_custom_call", output_to_operand_aliasing={{0}: (7, {}), {1}: (8, {})} | custom-call | tf_op jit(solution)/shard_map/finish/pallas_call | solution.py:344
Async XLA Ops:
  13.1 16.9 %collective-permute-start.1 = (bf16[2,2048,512]{2,1,0:T(8,128)(2,1)}, bf16[2,2048,512]{2,1,0:T(8,128)(2,1)}, u32[]{:S(2)}, u32[]{:S(2)}) collective-permute-start(bf16[2,2048,512]{2,1,0:T(8,128)(2,1)} %param.39), channel_id=1, source_target_pairs={{0,2},{2,0},{4,6},{6,4},{8,10},{10,8},{12,14},{14,12},{16,18},{18,... | collective-permute-start | bytes 12582920 | tf_op jit(solution)/shard_map/ppermute | solution.py:608
  13.6 16.4 %collective-permute-start.2 = (bf16[2,2048,512]{2,1,0:T(8,128)(2,1)}, bf16[2,2048,512]{2,1,0:T(8,128)(2,1)}, u32[]{:S(2)}, u32[]{:S(2)}) collective-permute-start(bf16[2,2048,512]{2,1,0:T(8,128)(2,1)} %param.40), channel_id=1, source_target_pairs={{0,2},{2,0},{4,6},{6,4},{8,10},{10,8},{12,14},{14,12},{16,18},{18,... | collective-permute-start | bytes 12582920 | tf_op jit(solution)/shard_map/ppermute | solution.py:608
  13.7 16.3 %collective-permute-start = (bf16[128,2048]{1,0:T(8,128)(2,1)}, bf16[128,2048]{1,0:T(8,128)(2,1)S(1)}, u32[]{:S(2)}, u32[]{:S(2)}) collective-permute-start(bf16[128,2048]{1,0:T(8,128)(2,1)} %get-tuple-element.29), channel_id=1, source_target_pairs={{0,1},{1,0},{2,3},{3,2},{4,5},{5,4},{6,7},{7,6},{8,9},{9,8},{10,11... | collective-permute-start | bytes 1572872 | tf_op jit(solution)/shard_map/ppermute | solution.py:614
  29.9 25.5 %collective-permute-start.4 = (bf16[192,2048]{1,0:T(8,128)(2,1)}, bf16[192,2048]{1,0:T(8,128)(2,1)S(1)}, u32[]{:S(2)}, u32[]{:S(2)}) collective-permute-start(bf16[192,2048]{1,0:T(8,128)(2,1)} %get-tuple-element.43), channel_id=1, source_target_pairs={{0,1},{1,0},{2,3},{3,2},{4,5},{5,4},{6,7},{7,6},{8,9},{9,8},{10,11... | collective-permute-start | bytes 2359304 | tf_op jit(solution)/shard_map/ppermute | solution.py:614
  42.0 19.8 %collective-permute-start.5 = (bf16[128,2048]{1,0:T(8,128)(2,1)}, bf16[128,2048]{1,0:T(8,128)(2,1)S(1)}, u32[]{:S(2)}, u32[]{:S(2)}) collective-permute-start(bf16[128,2048]{1,0:T(8,128)(2,1)} %get-tuple-element.46), channel_id=1, source_target_pairs={{0,1},{1,0},{2,3},{3,2},{4,5},{5,4},{6,7},{7,6},{8,9},{9,8},{10,11... | collective-permute-start | bytes 1572872 | tf_op jit(solution)/shard_map/ppermute | solution.py:614
  44.0 11.3 %copy-start = (f32[192,2048]{1,0:T(8,128)S(1)}, f32[192,2048]{1,0:T(8,128)}, u32[]{:S(2)}) copy-start(f32[192,2048]{1,0:T(8,128)} %get-tuple-element.44.refs_3_) | copy-start | bytes 4718596
  44.0 11.3 %copy-start.1 = (f32[128,2048]{1,0:T(8,128)S(1)}, f32[128,2048]{1,0:T(8,128)}, u32[]{:S(2)}) copy-start(f32[128,2048]{1,0:T(8,128)} %get-tuple-element.37.refs_2_) | copy-start | bytes 3145732
  44.0 11.3 %copy-start.4 = (f32[2048]{0:T(1024)S(1)}, f32[2048]{0:T(1024)}, u32[]{:S(2)}) copy-start(f32[2048]{0:T(1024)} %param.33) | copy-start | bytes 24580
  44.0 11.4 %copy-start.5 = (f32[2048]{0:T(1024)S(1)}, f32[2048]{0:T(1024)}, u32[]{:S(2)}) copy-start(f32[2048]{0:T(1024)} %param.34) | copy-start | bytes 24580
  44.0 11.4 %copy-start.6 = (f32[3,512]{1,0:T(4,128)S(1)}, f32[3,512]{1,0:T(4,128)}, u32[]{:S(2)}) copy-start(f32[3,512]{1,0:T(4,128)} %refs_5_.3) | copy-start | bytes 18436
  55.2 11.0 %collective-permute-start.3 = (bf16[64,2048]{1,0:T(8,128)(2,1)}, bf16[64,2048]{1,0:T(8,128)(2,1)S(1)}, u32[]{:S(2)}, u32[]{:S(2)}) collective-permute-start(bf16[64,2048]{1,0:T(8,128)(2,1)} %get-tuple-element.41), channel_id=1, source_target_pairs={{0,1},{1,0},{2,3},{3,2},{4,5},{5,4},{6,7},{7,6},{8,9},{9,8},{10,11... | collective-permute-start | bytes 786440 | tf_op jit(solution)/shard_map/ppermute | solution.py:614
  55.4 6.4 %copy-start.2 = (f32[128,2048]{1,0:T(8,128)S(1)}, f32[128,2048]{1,0:T(8,128)}, u32[]{:S(2)}) copy-start(f32[128,2048]{1,0:T(8,128)} %get-tuple-element.47.refs_1_) | copy-start | bytes 3145732
  61.8 4.4 %copy-start.3 = (f32[64,2048]{1,0:T(8,128)S(1)}, f32[64,2048]{1,0:T(8,128)}, u32[]{:S(2)}) copy-start(f32[64,2048]{1,0:T(8,128)} %get-tuple-element.42.refs_1_) | copy-start | bytes 1572868
